TPU v7x, 32 devices: a whole 2x2x4 slice. The times are simulated.
32 devices in a mesh: wide: 8 (over z, x), narrow: 4 (over y, core).
Axes of the slice: x: 2, y: 2, z: 4, core: 2. Of those that a mesh axis runs over, the one named last changes fastest.
Arguments:
- tokens: bfloat16 [26880, 768], P(('wide', 'narrow')), may hold values from -6 to 6
- patch_counts: int32 [96], P('wide'), may hold values from 100 to 240, as said below
- ln1_gain: float32 [768], replicated, may hold values from 0.25 to 1.75
- ln1_bias: float32 [768], replicated, may hold values from -3 to 3
- w_qkv: bfloat16 [768, 3, 768], P(None, None, 'narrow'), may hold values from -0.21875 to 0.21875
- b_qv: float32 [2, 768], P(None, 'narrow'), may hold values from -3 to 3
- w_out: bfloat16 [768, 768], P('narrow'), may hold values from -0.625 to 0.625
- b_out: float32 [768], replicated, may hold values from -3 to 3
- ln2_gain: float32 [768], replicated, may hold values from 0.25 to 1.75
- ln2_bias: float32 [768], replicated, may hold values from -3 to 3
- w_up: bfloat16 [768, 3072], P(None, 'narrow'), may hold values from -0.21875 to 0.21875
- b_up: bfloat16 [1, 3072], P(None, 'narrow'), may hold values from -3 to 3
- w_down: bfloat16 [3072, 768], P('narrow'), may hold values from -0.109375 to 0.109375
- b_down: float32 [768], replicated, may hold values from -3 to 3
- cotangent: bfloat16 [26880, 768], P(('wide', 'narrow')), may hold values from -6 to 6
Outputs:
- layer_out: float32 [26880, 768], P(('wide', 'narrow'))
- input_grad: float32 [26880, 768], P(('wide', 'narrow'))
- ln1_gain_grad: float32 [768], replicated
- ln1_bias_grad: float32 [768], replicated
- w_qkv_grad: float32 [768, 3, 768], P(None, None, 'narrow')
- b_qv_grad: float32 [2, 768], P(None, 'narrow')
- w_out_grad: float32 [768, 768], P('narrow')
- b_out_grad: float32 [768], replicated
- ln2_gain_grad: float32 [768], replicated
- ln2_bias_grad: float32 [768], replicated
- w_up_grad: float32 [768, 3072], P(None, 'narrow')
- b_up_grad: float32 [1, 3072], P(None, 'narrow')
- w_down_grad: float32 [3072, 768], P('narrow')
- b_down_grad: float32 [768], replicated
Inputs may be any that keep to these rules, and one draw needn't show every extreme that they name: patch_counts[i] is the number of real patches of item i; key positions 40 + patch_counts[i] and later of that item are padding.
All inputs are finite; a program needn't handle non-finite values.
Results may differ from a plain program's by a relative error of at most 0.012.
The roundings to bfloat16 on the way count: a program that leaves them out, or rounds other values in their place, can miss the bound.
Values may be sent and summed in bfloat16 or wider, within the bound.
No kernel may reach another device: no remote copies, remote signals or barrier semaphores. Data moves between devices by JAX's collectives and lax.ppermute only.
A program may use at most 192 MiB of HBM per device.

v0:
```python
import functools

import jax
import jax.numpy as jnp
from jax import lax
from jax.experimental import pallas as pl
from jax.experimental.pallas import tpu as pltpu
from jax.sharding import PartitionSpec as P

HEAD = 64
WORDS = 40
PACK = 16
LANES = 128
BLOCK = 256

norm_eps = 1e-06
masked_value = -1000000000.0
bf = jnp.bfloat16
f32 = jnp.float32


def mul_nn(a, b):
    return lax.dot_general(a, b, (((1,), (0,)), ((), ())), preferred_element_type=f32)


def mul_nt(a, b):
    return lax.dot_general(a, b, (((1,), (1,)), ((), ())), preferred_element_type=f32)


def mul_tn(a, b):
    return lax.dot_general(a, b, (((0,), (0,)), ((), ())), preferred_element_type=f32)


def pad_rows(x, rows):
    if x.shape[0] == rows:
        return x
    return jnp.concatenate([x, jnp.zeros((rows - x.shape[0],) + x.shape[1:], x.dtype)], axis=0)


def unit_parts(x):
    centred = x - jnp.mean(x, axis=-1, keepdims=True)
    inv = lax.rsqrt(jnp.mean(centred * centred, axis=-1, keepdims=True) + norm_eps)
    return centred * inv, inv


def norm_back(grad, unit, inv, gain):
    scaled = grad * gain
    inner = (
        scaled
        - jnp.mean(scaled, axis=-1, keepdims=True)
        - unit * jnp.mean(scaled * unit, axis=-1, keepdims=True)
    )
    return inv * inner


def col_sum(x):
    return jnp.sum(x, axis=0, keepdims=True)


def full(shape):
    return pl.BlockSpec(shape, lambda *_: (0,) * len(shape))


def per_item(shape):
    return pl.BlockSpec((None,) + shape, lambda i, *_: (i,) + (0,) * len(shape))


TIMES = {
    "attend": 10,
    "branch": 3,
    "feed": 18,
    "project": 6,
    "unbranch": 6,
    "unattend": 11,
    "unnorm": 6,
}


def lasting(us):
    return pl.CostEstimate(flops=int(us * 1.15e9), bytes_accessed=0, transcendentals=0)


def params(mib):
    return pltpu.CompilerParams(vmem_limit_bytes=mib << 20)


def two_rows(w_one, w_two, c):
    return jnp.concatenate([w_one[c], w_two[c]], axis=0)


def attend_kernel(first, counts, tokens, small, w_one, w_two, b_one, b_two, *outs):
    if first:
        q_out, k_out, v_out, mixed_out, log_out, normed_out = outs
    else:
        q_out, k_out, v_out, mixed_out, log_out = outs
    rows, width = q_out.shape
    unit, _ = unit_parts(pad_rows(tokens[...].astype(f32), rows))
    normed = (unit * small[0:1] + small[1:2]).astype(bf)
    b = jnp.concatenate([b_one[...], b_two[...]], axis=1)
    if first:
        normed_out[...] = normed
    q = ((mul_nt(normed, two_rows(w_one, w_two, 0)) + b[0:1]) * 0.125).astype(bf)
    k = mul_nt(normed, two_rows(w_one, w_two, 1)).astype(bf)
    v = (mul_nt(normed, two_rows(w_one, w_two, 2)) + b[1:2]).astype(bf)
    q_out[...] = q
    k_out[...] = k
    v_out[...] = v
    valid = WORDS + counts[pl.program_id(0)]
    mask = jnp.where(lax.broadcasted_iota(jnp.int32, (1, rows), 1) < valid, 0.0, masked_value)
    lane = lax.broadcasted_iota(jnp.int32, (rows, LANES), 1)
    low = lane < HEAD
    logs = jnp.zeros((rows, LANES), f32)
    for p in range(width // LANES):
        at = slice(p * LANES, (p + 1) * LANES)
        q_two, k_two, v_two = q[:, at], k[:, at], v[:, at]
        tops, sums = [], []
        for h in range(2):
            here = low if h == 0 else ~low
            scores = mul_nt(jnp.where(here, q_two, 0), k_two) + mask
            top = jnp.max(scores, axis=1, keepdims=True)
            shifted = jnp.exp(scores - top).astype(bf)
            sums.append(mul_nn(shifted, jnp.where(here, v_two, 1)))
            tops.append(top)
        total = pltpu.roll(jnp.where(low, sums[1], sums[0]), HEAD, 1)
        mixed_out[:, at] = (jnp.where(low, sums[0], sums[1]) / total).astype(bf)
        log_two = jnp.log(total)
        logs = jnp.where(lane == 2 * p, tops[0] + log_two[:, 0:1], logs)
        logs = jnp.where(lane == 2 * p + 1, tops[1] + log_two[:, HEAD : HEAD + 1], logs)
    log_out[...] = logs.T[: log_out.shape[0]]


def attend(first, counts, tokens, small, ws, bs, rows):
    items, _, dim = tokens.shape
    width = 2 * ws[0].shape[1]
    wide_out = jax.ShapeDtypeStruct((items, rows, width), bf)
    outs = [wide_out] * 4 + [jax.ShapeDtypeStruct((items, 8, rows), f32)]
    specs = [per_item((rows, width))] * 4 + [per_item((8, rows))]
    if first:
        outs.append(jax.ShapeDtypeStruct((items, rows, dim), bf))
        specs.append(per_item((rows, dim)))
    return pl.pallas_call(
        functools.partial(attend_kernel, first),
        grid_spec=pltpu.PrefetchScalarGridSpec(
            num_scalar_prefetch=1,
            grid=(items,),
            in_specs=[
                per_item(tokens.shape[1:]),
                full(small.shape),
                full(ws[0].shape),
                full(ws[0].shape),
                full(bs[0].shape),
                full(bs[0].shape),
            ],
            out_specs=specs,
        ),
        out_shape=outs,
        compiler_params=params(8),
        cost_estimate=lasting(TIMES["attend"]),
        name="attend",
    )(counts, tokens, small, *ws, *bs)


def branch_kernel(tokens, cot, mixed_a, mixed_b, w_a, w_b, small, middle_out, normed_out, cot_out):
    rows = normed_out.shape[0]
    middle = (
        pad_rows(tokens[...].astype(f32), rows)
        + (mul_nn(mixed_a[...], w_a[...]) + mul_nn(mixed_b[...], w_b[...]))
        + small[2:3]
    )
    middle_out[...] = middle
    unit, _ = unit_parts(middle)
    normed_out[...] = (unit * small[3:4] + small[4:5]).astype(bf)
    cot_out[...] = pad_rows(cot[...].astype(f32), rows).astype(bf)


def branch(tokens, cot, mixed_a, mixed_b, w_a, w_b, small):
    items, seq, dim = tokens.shape
    _, rows, width = mixed_a.shape
    return pl.pallas_call(
        branch_kernel,
        grid=(items,),
        in_specs=[per_item((seq, dim))] * 2
        + [per_item((rows, width))] * 2
        + [full(w_a.shape)] * 2
        + [full(small.shape)],
        out_specs=[per_item((rows, dim))] * 3,
        out_shape=[
            jax.ShapeDtypeStruct((items, rows, dim), f32),
            jax.ShapeDtypeStruct((items, rows, dim), bf),
            jax.ShapeDtypeStruct((items, rows, dim), bf),
        ],
        compiler_params=params(7),
        cost_estimate=lasting(TIMES["branch"]),
        name="branch",
    )(tokens, cot, mixed_a, mixed_b, w_a, w_b, small)


def feed_kernel(
    again, per, low_half, normed, cot, base_grad, *refs
):
    n_weights = 6 if again else 4
    weights, rest = refs[:n_weights], refs[n_weights:]
    bias_a, bias_b, grad_ref, hidden_ref, dup_a, dup_b, ddown_a, ddown_b, dbias_ref, gu_ref = rest
    step = pl.program_id(0)
    items, rows, dim = normed.shape
    is_a = step < per

    @pl.when(step == 0)
    def _():
        grad_ref[...] = base_grad[...] if again else jnp.zeros_like(grad_ref)

    if again:
        up_a, up_b, up_c, up_d, down_a, down_c = weights
        is_low = low_half[0] == 0
        first = jnp.where(is_a, up_a[...], up_c[...])
        second = jnp.where(is_a, up_b[...], up_d[...])
        w_up = jnp.concatenate(
            [jnp.where(is_low, first, second), jnp.where(is_low, second, first)], axis=0
        )
    else:
        up_a, up_c, down_a, down_c = weights
        w_up = jnp.where(is_a, up_a[...], up_c[...])
    w_down = jnp.where(is_a, down_a[...], down_c[...])
    bias = jnp.where(is_a, bias_a[...].astype(f32), bias_b[...].astype(f32))
    bias_sum = jnp.zeros((1, w_up.shape[1]), f32)
    for i in range(items):
        up = mul_nn(normed[i], w_up) + bias
        grad_hidden = mul_nt(cot[i], w_down)
        cdf = 0.5 * (1.0 + lax.erf(up * 0.7071067811865476))
        slope = cdf + up * (jnp.exp(-0.5 * up * up) * 0.3989422804014327)
        gu = (slope * grad_hidden).astype(bf)
        hidden_ref[i] = (up * cdf).astype(bf)
        gu_ref[i] = gu
        bias_sum = bias_sum + col_sum(gu.astype(f32))
        grad_ref[i] += mul_nt(gu, w_up)
    dbias_ref[...] = bias_sum
    flat = (items * rows, dim)
    hidden = hidden_ref[...].reshape(items * rows, -1)
    gu = gu_ref[...].reshape(items * rows, -1)
    ddown = mul_tn(hidden, cot[...].reshape(flat)).astype(bf)
    dup = mul_tn(normed[...].reshape(flat), gu).astype(bf)

    @pl.when(is_a)
    def _():
        ddown_a[...] = ddown
        dup_a[...] = dup

    @pl.when(jnp.logical_not(is_a))
    def _():
        ddown_b[...] = ddown
        dup_b[...] = dup


def feed(low_half, normed, cot, base_grad, ups, downs, biases):
    again = base_grad is not None
    items, rows, dim = normed.shape
    units = ups[0].shape[1]
    per = units // BLOCK
    steps = 2 * per
    full3 = full((items, rows, dim))
    if not again:
        base_grad = biases[0]
    half = len(ups) // 2
    first = lambda j: jnp.minimum(j, per - 1)
    second = lambda j: jnp.maximum(j - per, 0)
    across = lambda part, place: pl.BlockSpec((part, BLOCK), lambda j, *_: (0, place(j)))
    down = lambda place: pl.BlockSpec((BLOCK, dim), lambda j, *_: (place(j), 0))
    return pl.pallas_call(
        functools.partial(feed_kernel, again, per),
        grid_spec=pltpu.PrefetchScalarGridSpec(
            num_scalar_prefetch=1,
            grid=(steps,),
            in_specs=[full3, full3, full3 if again else full(base_grad.shape)]
            + [across(dim // half, first)] * half
            + [across(dim // half, second)] * half
            + [down(first), down(second)]
            + [across(1, first), across(1, second)],
            out_specs=[
                full3,
                pl.BlockSpec((items, rows, BLOCK), lambda j, *_: (0, 0, j)),
                across(dim, first),
                across(dim, second),
                down(first),
                down(second),
                pl.BlockSpec((1, BLOCK), lambda j, *_: (0, j)),
            ],
            scratch_shapes=[pltpu.VMEM((items, rows, BLOCK), bf)],
        ),
        out_shape=[
            jax.ShapeDtypeStruct((items, rows, dim), f32),
            jax.ShapeDtypeStruct((items, rows, 2 * units), bf),
            jax.ShapeDtypeStruct((dim, units), bf),
            jax.ShapeDtypeStruct((dim, units), bf),
            jax.ShapeDtypeStruct((units, dim), bf),
            jax.ShapeDtypeStruct((units, dim), bf),
            jax.ShapeDtypeStruct((1, 2 * units), f32),
        ],
        compiler_params=params(14),
        cost_estimate=lasting(TIMES["feed"]),
        name="feed",
    )(low_half, normed, cot, base_grad, *ups, *downs, *biases)


def project_kernel(middle, small, hidden_a, hidden_b, *refs):
    weights, out_ref = refs[:4], refs[4]
    units = weights[0].shape[0]
    total = middle[...] + small[5:6]
    for n, w in enumerate(weights):
        hidden = (hidden_a, hidden_b)[n // 2]
        total = total + mul_nn(hidden[:, (n % 2) * units : (n % 2 + 1) * units], w[...])
    out_ref[...] = total[: out_ref.shape[0]]


def project(middle, small, hidden_a, hidden_b, weights, seq):
    items, rows, dim = middle.shape
    both = per_item(hidden_a.shape[1:])
    return pl.pallas_call(
        project_kernel,
        grid=(items,),
        in_specs=[per_item((rows, dim)), full(small.shape), both, both] + [full(weights[0].shape)] * 4,
        out_specs=per_item((seq, dim)),
        out_shape=jax.ShapeDtypeStruct((items, seq, dim), f32),
        compiler_params=params(14),
        cost_estimate=lasting(TIMES["project"]),
        name="project",
    )(middle, small, hidden_a, hidden_b, *weights)


def unbranch_kernel(
    middle, cot, grad_in, vectors, mixed_a, mixed_b, w_a, w_b,
    grad_out, gmix_a, gmix_b, dw_out, small, branch_ref
):
    step = pl.program_id(0)
    unit, inv = unit_parts(middle[...])
    grad = grad_in[...]
    cot_f = cot[...].astype(f32)
    grad_middle = cot_f + norm_back(grad, unit, inv, vectors[3:4])
    grad_out[...] = grad_middle
    grad_branch = grad_middle.astype(bf)
    branch_ref[step] = grad_branch
    gmix_a[...] = mul_nt(grad_branch, w_a[...]).astype(bf)
    gmix_b[...] = mul_nt(grad_branch, w_b[...]).astype(bf)

    @pl.when(step == 0)
    def _():
        small[...] = jnp.zeros_like(small)

    small[0:1] += col_sum(grad * unit)
    small[1:2] += col_sum(grad)
    small[2:3] += col_sum(grad_branch.astype(f32))
    small[3:4] += col_sum(cot_f)

    @pl.when(step == pl.num_programs(0) - 1)
    def _():
        items, rows, dim = branch_ref.shape
        gb = branch_ref[...].reshape(items * rows, dim)
        width = mixed_a.shape[2]
        quarter = width // 2
        for n, mixed in ((0, mixed_a), (1, mixed_b)):
            dw = mul_tn(mixed[...].reshape(items * rows, width), gb).astype(bf)
            dw_out[2 * n] = dw[:quarter]
            dw_out[2 * n + 1] = dw[quarter:]


def unbranch(middle, cot, grad_in, vectors, mixed_a, mixed_b, w_a, w_b):
    items, rows, dim = middle.shape
    width = mixed_a.shape[2]
    each = per_item((rows, dim))
    return pl.pallas_call(
        unbranch_kernel,
        grid=(items,),
        in_specs=[each, each, each, full(vectors.shape)]
        + [full(mixed_a.shape)] * 2
        + [full(w_a.shape)] * 2,
        out_specs=[
            each,
            per_item((rows, width)),
            per_item((rows, width)),
            full((4, width // 2, dim)),
            full((8, dim)),
        ],
        out_shape=[
            jax.ShapeDtypeStruct((items, rows, dim), f32),
            jax.ShapeDtypeStruct((items, rows, width), bf),
            jax.ShapeDtypeStruct((items, rows, width), bf),
            jax.ShapeDtypeStruct((4, width // 2, dim), bf),
            jax.ShapeDtypeStruct((8, dim), f32),
        ],
        scratch_shapes=[pltpu.VMEM((items, rows, dim), bf)],
        compiler_params=params(12),
        cost_estimate=lasting(TIMES["unbranch"]),
        name="unbranch",
    )(middle, cot, grad_in, vectors, mixed_a, mixed_b, w_a, w_b)


def unattend_kernel(counts, q, k, v, gmix, logs, normed, g_ref, dw_out, db_out):
    step = pl.program_id(0)
    rows, width = q.shape
    valid = WORDS + counts[step]
    mask = jnp.where(lax.broadcasted_iota(jnp.int32, (rows, 1), 0) < valid, 0.0, masked_value)
    low = lax.broadcasted_iota(jnp.int32, (rows, LANES), 1) < HEAD
    def one_pair(p, carry):
        at = pl.ds(pl.multiple_of(p * LANES, LANES), LANES)
        q_two, k_two, v_two, g_two = q[:, at], k[:, at], v[:, at], gmix[:, at]
        dq, dk, dv = [], [], []
        for h in range(2):
            here = low if h == 0 else ~low
            scores = mul_nt(jnp.where(here, k_two, 0), q_two) + mask
            prob = jnp.exp(scores - logs[pl.ds(2 * p + h, 1)])
            grad_prob = mul_nt(jnp.where(here, v_two, 0), g_two)
            inner = jnp.sum(grad_prob * prob, axis=0, keepdims=True)
            grad_scores = (prob * (grad_prob - inner)).astype(bf)
            dv.append(mul_nn(prob.astype(bf), g_two))
            dk.append(mul_nn(grad_scores, q_two))
            dq.append(mul_tn(grad_scores, k_two))
        for c, pair in enumerate((dq, dk, dv)):
            merged = jnp.where(low, pair[0], pair[1]).astype(bf)
            if c == 0:
                merged = merged * jnp.asarray(0.125, bf)
            g_ref[step, :, pl.ds(pl.multiple_of(c * width + p * LANES, LANES), LANES)] = merged
        return carry

    lax.fori_loop(0, width // LANES, one_pair, 0)

    @pl.when(step == 0)
    def _():
        db_out[...] = jnp.zeros_like(db_out)

    db_out[0:1] += col_sum(g_ref[step, :, :width].astype(f32))
    db_out[1:2] += col_sum(g_ref[step, :, 2 * width :].astype(f32))

    @pl.when(step == pl.num_programs(0) - 1)
    def _():
        items, _, dim = normed.shape
        flat = normed[...].reshape(items * rows, dim)
        quarter = width // 2
        for c in range(3):
            g = g_ref[:, :, c * width : (c + 1) * width].reshape(items * rows, width)
            dw = mul_tn(g, flat).astype(bf)
            dw_out[0, c] = dw[:quarter]
            dw_out[1, c] = dw[quarter:]


def unattend(counts, q, k, v, gmix, logs, normed):
    items, rows, width = q.shape
    dim = normed.shape[2]
    return pl.pallas_call(
        unattend_kernel,
        grid_spec=pltpu.PrefetchScalarGridSpec(
            num_scalar_prefetch=1,
            grid=(items,),
            in_specs=[per_item((rows, width))] * 4 + [per_item((8, rows)), full(normed.shape)],
            out_specs=[
                full((items, rows, 3 * width)),
                full((2, 3, width // 2, dim)),
                full((8, width)),
            ],
        ),
        out_shape=[
            jax.ShapeDtypeStruct((items, rows, 3 * width), bf),
            jax.ShapeDtypeStruct((2, 3, width // 2, dim), bf),
            jax.ShapeDtypeStruct((8, width), f32),
        ],
        compiler_params=params(12),
        cost_estimate=lasting(TIMES["unattend"]),
        name="unattend",
    )(counts, q, k, v, gmix, logs, normed)


def unnorm_kernel(g_a, g_b, w_one, w_two, w_three, w_four, tokens, vectors, grad_middle, x_out, small):
    rows = g_a.shape[0]
    grad = 0.0
    for g, one, two in ((g_a, w_one, w_two), (g_b, w_three, w_four)):
        w = jnp.concatenate([two_rows(one, two, c) for c in range(3)], axis=0)
        grad = grad + mul_nn(g[...], w)
    unit, inv = unit_parts(pad_rows(tokens[...].astype(f32), rows))

    @pl.when(pl.program_id(0) == 0)
    def _():
        small[...] = jnp.zeros_like(small)

    small[0:1] += col_sum(grad * unit)
    small[1:2] += col_sum(grad)
    x_out[...] = (grad_middle[...] + norm_back(grad, unit, inv, vectors[0:1]))[: x_out.shape[0]]


def unnorm(g_a, g_b, ws, tokens, vectors, grad_middle):
    items, rows, width3 = g_a.shape
    seq, dim = tokens.shape[1:]
    return pl.pallas_call(
        unnorm_kernel,
        grid=(items,),
        in_specs=[per_item((rows, width3))] * 2
        + [full(ws[0].shape)] * 4
        + [per_item((seq, dim)), full(vectors.shape), per_item((rows, dim))],
        out_specs=[per_item((seq, dim)), full((8, dim))],
        out_shape=[
            jax.ShapeDtypeStruct((items, seq, dim), f32),
            jax.ShapeDtypeStruct((8, dim), f32),
        ],
        compiler_params=params(12),
        cost_estimate=lasting(TIMES["unnorm"]),
        name="unnorm",
    )(g_a, g_b, *ws, tokens, vectors, grad_middle)


def outer_kernel(g, normed, dw_out):
    items, rows, dim = normed.shape
    dw = mul_tn(g[...].reshape(items * rows, -1), normed[...].reshape(items * rows, dim)).astype(bf)
    quarter = dw.shape[0] // 2
    dw_out[0] = dw[:quarter]
    dw_out[1] = dw[quarter:]


def outer(g, normed):
    items, rows, width3 = g.shape
    dim = normed.shape[2]
    width = width3 // 3
    return pl.pallas_call(
        outer_kernel,
        grid=(3,),
        in_specs=[pl.BlockSpec((items, rows, width), lambda c: (0, 0, c)), full(normed.shape)],
        out_specs=pl.BlockSpec((2, None, width // 2, dim), lambda c: (0, c, 0, 0)),
        out_shape=jax.ShapeDtypeStruct((2, 3, width // 2, dim), bf),
        compiler_params=params(10),
        cost_estimate=lasting(TIMES["outer"]),
        name="outer",
    )(g, normed)


def exchange(x, axis, size, mask):
    return lax.ppermute(x, axis, [(i, i ^ mask) for i in range(size)])


def tie(*values):
    return lax.optimization_barrier(values)


def add_bf(*parts):
    total = parts[0].astype(f32)
    for part in parts[1:]:
        total = total + part.astype(f32)
    return total.astype(bf)


def piece(x, index, count):
    rows = x.shape[0] // count
    return lax.dynamic_slice_in_dim(x, index * rows, rows, 0)


class Wide:
    def __init__(self, size):
        self.size = size
        self.me = lax.axis_index("wide")
        self.groups = [(1, 2)]
        bit = 2
        while bit < size:
            self.groups.append((bit, min(4, size // bit)))
            bit *= self.groups[-1][1]

    def send(self, group, x):
        bit, members = group
        mine = (self.me // bit) % members
        got = [
            exchange(piece(x, mine ^ k, members), "wide", self.size, bit * k)
            for k in range(1, members)
        ]
        return [piece(x, mine, members)] + got

    def gathered(self, group, x):
        bit, members = group
        return [x] + [exchange(x, "wide", self.size, bit * k) for k in range(1, members)]

    def place(self, group, pieces):
        bit, members = group
        mine = (self.me // bit) % members
        if members == 2:
            low = mine == 0
            x, got = pieces
            return jnp.concatenate([jnp.where(low, x, got), jnp.where(low, got, x)], axis=0)
        x = pieces[0]
        rows = x.shape[0]
        out = jnp.zeros((members * rows,) + x.shape[1:], x.dtype)
        for k, part in enumerate(pieces):
            out = lax.dynamic_update_slice_in_dim(out, part, (mine ^ k) * rows, 0)
        return out

    def gather(self, group, x):
        return self.place(group, self.gathered(group, x))

    def over(self, groups, x):
        for group in groups:
            x = add_bf(*self.send(group, x))
        return x

    def back(self, groups, x):
        for group in reversed(groups):
            x = self.gather(group, x)
        return x


def on_device(
    wide,
    narrow,
    tokens,
    patch_counts,
    ln1_gain,
    ln1_bias,
    w_qkv,
    b_qv,
    w_out,
    b_out,
    ln2_gain,
    ln2_bias,
    w_up,
    b_up,
    w_down,
    b_down,
    cotangent,
):
    own_rows, dim = tokens.shape
    items = patch_counts.shape[0] // narrow
    seq = own_rows // items
    rows = -(-seq // PACK) * PACK
    heads = w_qkv.shape[2]
    units = w_up.shape[1]
    me = lax.axis_index("narrow")
    counts = lax.dynamic_slice_in_dim(patch_counts, me * items, items, 0)
    tokens3 = tokens.reshape(items, seq, dim)
    cot3 = cotangent.reshape(items, seq, dim)
    mate = lambda x: exchange(x, "narrow", narrow, 1)
    peer = lambda x: exchange(x, "narrow", narrow, 2)

    ring = Wide(wide)
    across = lambda x: exchange(x, "wide", wide, 1)
    x_axis, z_axis, more = ring.groups[0], ring.groups[1], ring.groups[2:]
    low_half = (ring.me % 2).astype(jnp.int32)
    half_dim = dim // 2

    w_own = w_qkv.transpose(1, 2, 0)
    w_peer, w_mate = peer(w_own), mate(w_own)
    b_peer, b_mate = peer(b_qv), mate(b_qv)
    vectors = jnp.concatenate([ln1_gain, ln1_bias, b_out, ln2_gain, ln2_bias, b_down]).reshape(6, dim)
    w_a = [w_own, w_mate]
    q_a, k_a, v_a, mixed_a, log_a, normed1 = attend(
        True, counts, tokens3, vectors, w_a, [b_qv, b_mate], rows
    )

    log_a, out_later, w_up, w_down, b_up = tie(log_a, w_out, w_up, w_down, b_up)
    out_peer, bias_peer = peer(out_later), peer(b_up)
    out_mate, bias_mate = mate(out_later), mate(b_up)
    up_mate, down_mate = mate(w_up), mate(w_down)
    up_part = lax.dynamic_slice_in_dim(w_up, low_half * half_dim, half_dim, 0)
    log_a, w_peer, b_peer, up_part = tie(log_a, w_peer, b_peer, up_part)
    up_first = peer(up_part)
    w_b = [w_peer, mate(w_peer)]
    q_b, k_b, v_b, mixed_b, log_b = attend(
        False, counts, tokens3, vectors, w_b, [b_peer, mate(b_peer)], rows
    )
    mixed_b, out_peer, up_first, down_later = tie(mixed_b, out_peer, up_first, w_down)
    down_peer = peer(down_later)
    out_a = jnp.concatenate([w_out, out_mate], axis=0)
    out_b = jnp.concatenate([out_peer, mate(out_peer)], axis=0)
    middle, normed2, cot_pad = branch(
        tokens3, cot3, mixed_a, mixed_b, out_a, out_b, vectors
    )
    middle, normed2, cot_pad, up_first = tie(middle, normed2, cot_pad, up_first)
    up_second, up_first_far = across(up_first), mate(up_first)
    flag = low_half.reshape(1)
    grad_part, hidden_a, dup_own, dup_mate, ddown_own, ddown_mate, dbias_a = feed(
        flag, normed2, cot_pad, None, [w_up, up_mate], [w_down, down_mate], [b_up, bias_mate]
    )

    grad_part, dup_own, dup_mate, ddown_own, ddown_mate, up_second, up_first_far = tie(
        grad_part, dup_own, dup_mate, ddown_own, ddown_mate, up_second, up_first_far
    )
    got_up, got_down = mate(dup_mate), mate(ddown_mate)
    up_second_far = mate(up_second)
    grad_part, down_peer = tie(grad_part, down_peer)
    ups = [up_first, up_second, up_first_far, up_second_far]
    downs = [down_peer, mate(down_peer)]
    grad_norm2, hidden_b, dup_peer, dup_far, ddown_peer, ddown_far, dbias_b = feed(
        flag, normed2, cot_pad, grad_part, ups, downs, [bias_peer, mate(bias_peer)]
    )
    grad_norm2, dup_peer, dup_far, ddown_peer, ddown_far, got_up, got_down = tie(
        grad_norm2, dup_peer, dup_far, ddown_peer, ddown_far, got_up, got_down
    )
    far_up, far_down = mate(dup_far), mate(ddown_far)
    grad_middle, gmix_a, gmix_b, dw_out, small_two = unbranch(
        middle, cot_pad, grad_norm2, vectors, mixed_a, mixed_b, out_a, out_b
    )

    grad_middle, gmix_a, gmix_b, dw_out, small_two, far_up, far_down = tie(
        grad_middle, gmix_a, gmix_b, dw_out, small_two, far_up, far_down
    )
    top = lambda x: x[:half_dim]
    bottom = lambda x: x[half_dim:]
    up_one = peer(add_bf(top(dup_peer), top(far_up)))
    pair_keep, pair_got = ring.send(x_axis, add_bf(ddown_peer, far_down))
    out_far, out_near = mate(dw_out[3]), mate(dw_out[1])
    g_b, dqkv_b, dbqv_b = unattend(counts, q_b, k_b, v_b, gmix_b, log_b, normed1)
    g_b, dqkv_b, dbqv_b, up_one, pair_keep, pair_got, ddown_own, got_down, out_far, out_near, far_up, dup_peer = tie(
        g_b, dqkv_b, dbqv_b, up_one, pair_keep, pair_got, ddown_own, got_down, out_far, out_near, far_up, dup_peer
    )
    down_keep, down_got = ring.send(x_axis, add_bf(ddown_own, got_down))

    def block(n, dqkv, dbqv, dbias):
        at = n % 2
        tail = [
            small_two[0:4],
            dbias[:, at * units : (at + 1) * units],
            jnp.pad(dbqv[0:2, at * heads : (at + 1) * heads], ((0, 0), (0, dim - heads))),
        ]
        tail = jnp.concatenate(tail, axis=0)
        pad = -(3 * heads + tail.shape[0]) % (8 * wide)
        tail = jnp.pad(tail, ((0, pad), (0, 0))).astype(bf)
        return jnp.concatenate([dqkv[at].reshape(3 * heads, dim), tail], axis=0)

    far_rest = mate(block(3, dqkv_b, dbqv_b, dbias_b))
    pair_half = peer(add_bf(pair_keep, pair_got))
    one_keep, one_got = ring.send(x_axis, add_bf(top(dup_own), top(got_up), up_one))
    vectors_late, dbqv_b = tie(vectors, dbqv_b)
    layer_out = project(middle, vectors_late, hidden_a, hidden_b, [w_down, down_mate] + downs, seq)
    gmix_a, far_rest, pair_half, layer_out, down_keep, down_got = tie(
        gmix_a, far_rest, pair_half, layer_out, down_keep, down_got
    )
    two_got = peer(
        jnp.concatenate([add_bf(bottom(dup_peer), bottom(far_up)), add_bf(dw_out[2], out_far)], axis=0)
    )
    rest_keep, rest_got = ring.send(x_axis, add_bf(block(2, dqkv_b, dbqv_b, dbias_b), far_rest))
    down_parts = ring.send(z_axis, add_bf(down_keep, down_got, pair_half))
    g_a, dqkv_a, dbqv_a = unattend(counts, q_a, k_a, v_a, gmix_a, log_a, normed1)
    g_a, dqkv_a, dbqv_a, rest_keep, rest_got, one_keep, one_got, two_got, *down_parts = tie(
        g_a, dqkv_a, dbqv_a, rest_keep, rest_got, one_keep, one_got, two_got, *down_parts
    )

    rest_mate = mate(block(1, dqkv_a, dbqv_a, dbias_a))
    rest_half = peer(add_bf(rest_keep, rest_got))
    two_own = jnp.concatenate([add_bf(bottom(dup_own), bottom(got_up)), add_bf(dw_out[0], out_near)], axis=0)
    two_keep, two_got = ring.send(x_axis, add_bf(two_own, two_got))
    down_all = ring.gathered(z_axis, ring.back(more, ring.over(more, add_bf(*down_parts))))
    rest_own = add_bf(block(0, dqkv_a, dbqv_a, dbias_a), rest_mate)
    rest_own, g_a = tie(rest_own, g_a)
    rest_keep, rest_got = ring.send(x_axis, rest_own)
    input_grad, small_one = unnorm(g_a, g_b, w_a + w_b, tokens3, vectors, grad_middle)
    small_one, rest_keep, rest_got, rest_half, two_keep, two_got, *down_all = tie(
        small_one, rest_keep, rest_got, rest_half, two_keep, two_got, *down_all
    )
    down_sum = ring.place(z_axis, down_all)
    firsts = small_one[0:2]
    firsts = firsts + mate(firsts)
    firsts = firsts + peer(firsts)
    firsts = firsts + across(firsts)
    up_half = jnp.concatenate([add_bf(one_keep, one_got), add_bf(two_keep, two_got)], axis=0)
    rest_sum = add_bf(rest_keep, rest_got, rest_half)
    spot = lax.broadcasted_iota(jnp.int32, (rest_sum.shape[0], 1), 0) - (
        3 * heads + 7 - low_half * rest_sum.shape[0]
    )
    whole = firsts.astype(bf)
    rest_sum = jnp.where(spot == 0, whole[0:1], jnp.where(spot == 1, whole[1:2], rest_sum))
    rest_sum = ring.back(ring.groups, ring.over(ring.groups[1:], rest_sum))
    up_sum = ring.back(ring.groups, ring.over(ring.groups[1:], up_half))
    down_sum = ring.back([x_axis], down_sum)
    quarter = half_dim // 2
    parts = [up_sum[: up_sum.shape[0] // 2], up_sum[up_sum.shape[0] // 2 :]]
    up_sum = jnp.concatenate([x[:quarter] for x in parts] + [x[quarter:] for x in parts], axis=0)
    firsts = rest_sum[3 * heads + 7 : 3 * heads + 9].astype(f32)
    up_grad, out_grad = up_sum[:dim], up_sum[dim:]
    vec = rest_sum[3 * heads :].astype(f32)
    return (
        layer_out.reshape(own_rows, dim),
        input_grad.reshape(own_rows, dim),
        firsts[0],
        firsts[1],
        rest_sum[: 3 * heads].astype(f32).reshape(3, heads, dim).transpose(2, 0, 1),
        vec[5:7, :heads],
        out_grad.astype(f32),
        vec[2],
        vec[0],
        vec[1],
        up_grad.astype(f32),
        vec[4:5, :units],
        down_sum.astype(f32),
        vec[3],
    )


def solution(mesh):
    wide, narrow = mesh.shape["wide"], mesh.shape["narrow"]
    assert narrow == 4 and wide >= 4 and wide & (wide - 1) == 0
    rows = P(("wide", "narrow"), None)
    return jax.shard_map(
        functools.partial(on_device, wide, narrow),
        mesh=mesh,
        in_specs=(
            rows,
            P("wide"),
            P(),
            P(),
            P(None, None, "narrow"),
            P(None, "narrow"),
            P("narrow", None),
            P(),
            P(),
            P(),
            P(None, "narrow"),
            P(None, "narrow"),
            P("narrow", None),
            P(),
            rows,
        ),
        out_specs=(
            rows,
            rows,
            P(),
            P(),
            P(None, None, "narrow"),
            P(None, "narrow"),
            P("narrow", None),
            P(),
            P(),
            P(),
            P(None, "narrow"),
            P(None, "narrow"),
            P("narrow", None),
            P(),
        ),
        check_vma=False,
    )
```

profile of v0, /device:TPU:8, one launch (start us, length us, event | category | flops | bytes accessed | tf_op | source)
XLA Modules:
  0.0 281.1 jit_solution(13910026037448716387)
XLA Ops:
  11.4 10.5 %attend.2 = (bf16[3,288,384]{2,1,0:T(8,128)(2,1)S(1)}, bf16[3,288,384]{2,1,0:T(8,128)(2,1)S(1)}, bf16[3,288,384]{2,1,0:T(8,128)(2,1)S(1)}, bf16[3,288,384]{2,1,0...) custom-call(s32[3]{0:T(128)S(1)} %dynamic_slice.78.counts, ...), custom_call_target="tpu_custom_call" | custom-call | flops 11500000256 | tf_op jit(solution)/shard_map/attend/pallas_call | solution.py:141
  30.3 10.4 %attend.3 = (bf16[3,288,384]{2,1,0:T(8,128)(2,1)S(1)}, bf16[3,288,384]{2,1,0:T(8,128)(2,1)S(1)}, bf16[3,288,384]{2,1,0:T(8,128)(2,1)S(1)}, bf16[3,288,384]{2,1,0:T(8,128)(2,1)S(1)}, f32[3,8,288]{2,1,0:T(8,128)S(1)}) custom-call(s32[3]{0:T(128)S(1)} %dynamic_slice.78.counts, bf16[3,280,768]{2,1,0:T(8,128)(2,1)S(1)} %bitcast.26, ...), custom_call_target="tpu_custom_call" | custom-call | flops 11500000256 | tf_op jit(solution)/shard_map/attend/pallas_call | solution.py:141
  43.1 5.3 %collective-permute-done.7.refs_0_ = bf16[384,768]{1,0:T(8,128)(2,1)S(1)} collective-permute-done((bf16[384,768]{1,0:T(8,128)(2,1)S(1)}, bf16[384,768]{1,0:T(8,128)(2,1)S(1)}, u32[]{:S(2)}, u32[]{:S(2)}) %collective-permute-start.7) | collective-permute-done | bytes 589856 | tf_op jit(solution)/shard_map/ppermute | solution.py:532
  50.8 2.7 branch.1
  56.5 16.6 %feed.2 = (f32[3,288,768]{2,1,0:T(8,128)S(1)}, bf16[3,288,1536]{2,1,0:T(8,128)(2,1)S(1)}, bf16[768,768]{1,0:T(8,128)(2,1)S(1)}, bf16[768,768]{1,0:T(8,128)(2,1)S...) custom-call(s32[1]{0:T(128)} %bitcast.3.low_half, ...), custom_call_target="tpu_custom_call" | custom-call | flops 20700000256 | tf_op jit(solution)/shard_map/feed/pallas_call | solution.py:268
  80.6 2.7 collective-permute-done.18.refs_6_
  91.0 18.7 %feed.3 = (f32[3,288,768]{2,1,0:T(8,128)S(1)}, bf16[3,288,1536]{2,1,0:T(8,128)(2,1)S(1)}, bf16[768,768]{1,0:T(8,128)(2,1)S(1)}, bf16[768,768]{1,0:T(8,128)(2,1)S...) custom-call(s32[1]{0:T(128)} %bitcast.3.low_half, ...), custom_call_target="tpu_custom_call" | custom-call | flops 20700000256 | tf_op jit(solution)/shard_map/feed/pallas_call | solution.py:268
  110.4 5.9 %unbranch.1 = (f32[3,288,768]{2,1,0:T(8,128)S(1)}, bf16[3,288,384]{2,1,0:T(8,128)(2,1)S(1)}, bf16[3,288,384]{2,1,0:T(8,128)(2,1)S(1)}, bf16[4,192,768]{2,1,0:T(8,128)(2,1)S(1)}, f32[8,768]{1,0:T(8,128)S(1)}) custom-call(f32[3,288,768]{2,1,0:T(8,128)S(1)} %copy-done.30, bf16[3,288,768]{2,1,0:T(8,128)(2,1)S(1)} %copy-done.35, ...), custom_call_target="tpu_custom_call" | custom-call | flops 6899999744 | tf_op jit(solution)/shard_map/unbranch/pallas_call | solution.py:369
  119.7 11.9 %unattend.2 = (bf16[3,288,1152]{2,1,0:T(8,128)(2,1)S(1)}, bf16[2,3,192,768]{3,2,1,0:T(8,128)(2,1)S(1)}, f32[8,384]{1,0:T(8,128)S(1)}) custom-call(s32[3]{0:T(128)S(1)} %copy-done.28, bf16[3,288,384]{2,1,0:T(8,128)(2,1)S(1)} %copy-done.53, bf16[3,288,384]{2,1,0:T(8,128)(2,1)S(1)} %copy-done.55, bf16[3,288,384]{2,1,0:T(8,128)(2,1)S(1)} %copy-done.57, ...), custom_call_target="tpu_custom_call" | custom-call | flops 12650000384 | tf_op jit(solution)/shard_map/unattend/pallas_call | solution.py:447
  140.4 7.3 %project.1 = f32[3,280,768]{2,1,0:T(8,128)} custom-call(f32[3,288,768]{2,1,0:T(8,128)S(1)} %copy-done.30, f32[6,768]{1,0:T(8,128)S(1)} %copy-done.2, bf16[3,288,1536]{2,1,0:T(8,128)(2,1)S(1)} %copy-done.32, bf16[3,288,1536]{2,1,0:T(8,128)(2,1)S(1)} %get-tuple-element.211.hidden_b, bf16[768,768]{1,0:T(8,128)(2,1)S(1)} %copy-done.8, ...), custom_call_target="tpu_custom_call" | custom-call | flops 6899999744 | tf_op jit(solution)/shard_map/project/pallas_call | solution.py:317
  153.3 2.6 collective-permute-start.35
  159.4 11.9 %unattend.3 = (bf16[3,288,1152]{2,1,0:T(8,128)(2,1)S(1)}, bf16[2,3,192,768]{3,2,1,0:T(8,128)(2,1)S(1)}, f32[8,384]{1,0:T(8,128)S(1)}) custom-call(s32[3]{0:T(128)S(1)} %copy-done.28, bf16[3,288,384]{2,1,0:T(8,128)(2,1)S(1)} %copy-done.47, bf16[3,288,384]{2,1,0:T(8,128)(2,1)S(1)} %copy-done.49, bf16[3,288,384]{2,1,0:T(8,128)(2,1)S(1)} %copy-done.51, ...), custom_call_target="tpu_custom_call" | custom-call | flops 12650000384 | tf_op jit(solution)/shard_map/unattend/pallas_call | solution.py:447
  180.4 6.5 %unnorm.1 = (f32[3,280,768]{2,1,0:T(8,128)}, f32[8,768]{1,0:T(8,128)S(1)}) custom-call(bf16[3,288,1152]{2,1,0:T(8,128)(2,1)S(1)} %get-tuple-element.238.g_a, bf16[3,288,1152]{2,1,0:T(8,128)(2,1)S(1)} %get-tuple-element.239.g_b, bf16[3,192,768]{2,1,0:T(8,128)(2,1)S(1)} %bitcast.32, bf16[3,192,768]{2,1,0:T(8,128)(2,1)S(1)} %copy-done.16, ...), custom_call_target="tpu_custom_call" | custom-call | flops 6899999744 | tf_op jit(solution)/shard_map/unnorm/pallas_call | solution.py:490
  186.8 2.9 %collective-permute-done.43 = bf16[96,768]{1,0:T(8,128)(2,1)S(1)} collective-permute-done((bf16[96,768]{1,0:T(8,128)(2,1)S(1)}, bf16[96,768]{1,0:T(8,128)(2,1)S(1)}, u32[]{:S(2)}, u32[]{:S(2)}) %collective-permute-start.43) | collective-permute-done | bytes 147488 | tf_op jit(solution)/shard_map/ppermute | solution.py:532
  190.6 9.2 %collective-permute-done.38 = bf16[320,768]{1,0:T(8,128)(2,1)S(1)} collective-permute-done((bf16[320,768]{1,0:T(8,128)(2,1)S(1)}, bf16[320,768]{1,0:T(8,128)(2,1)S(1)}, u32[]{:S(2)}, u32[]{:S(2)}) %collective-permute-start.38) | collective-permute-done | bytes 491552 | tf_op jit(solution)/shard_map/ppermute | solution.py:532
  201.1 4.4 %collective-permute-start.55 = (bf16[120,768]{1,0:T(8,128)(2,1)S(1)}, bf16[120,768]{1,0:T(8,128)(2,1)S(1)}, u32[]{:S(2)}, u32[]{:S(2)}) collective-permute-start(bf16[120,768]{1,0:T(8,128)(2,1)S(1)} %get-tuple-element.305), channel_id=1, source_target_pairs={{0,16},{4,20},{8,24},{12,28},{16,0},{20,4},{24,8},{28,12},{1,17},{... | collective-permute-start | bytes 552968 | tf_op jit(solution)/shard_map/ppermute | solution.py:532
  209.8 3.1 %collective-permute-done.46 = f32[2,768]{1,0:T(2,128)S(1)} collective-permute-done((f32[2,768]{1,0:T(2,128)S(1)}, f32[2,768]{1,0:T(2,128)S(1)}, u32[]{:S(2)}, u32[]{:S(2)}) %collective-permute-start.46) | collective-permute-done | bytes 6176 | tf_op jit(solution)/shard_map/ppermute | solution.py:532
  214.2 2.6 collective-permute-start.47
  216.8 11.0 %collective-permute-done.49 = bf16[80,768]{1,0:T(8,128)(2,1)S(1)} collective-permute-done((bf16[80,768]{1,0:T(8,128)(2,1)S(1)}, bf16[80,768]{1,0:T(8,128)(2,1)S(1)}, u32[]{:S(2)}, u32[]{:S(2)}) %collective-permute-start.49) | collective-permute-done | bytes 122912 | tf_op jit(solution)/shard_map/ppermute | solution.py:532
  228.7 3.6 %collective-permute-start.50 = (bf16[80,768]{1,0:T(8,128)(2,1)S(1)}, bf16[80,768]{1,0:T(8,128)(2,1)S(1)}, u32[]{:S(2)}, u32[]{:S(2)}) collective-permute-start(bf16[80,768]{1,0:T(8,128)(2,1)S(1)} %get-tuple-element.275), channel_id=1, source_target_pairs={{0,8},{4,12},{8,0},{12,4},{16,24},{20,28},{24,16},{28,20},{1,9},{5... | collective-permute-start | bytes 368648 | tf_op jit(solution)/shard_map/ppermute | solution.py:532
  237.9 2.6 collective-permute-start.58
  242.7 11.1 %collective-permute-done.52 = bf16[80,768]{1,0:T(8,128)(2,1)S(1)} collective-permute-done((bf16[80,768]{1,0:T(8,128)(2,1)S(1)}, bf16[80,768]{1,0:T(8,128)(2,1)S(1)}, u32[]{:S(2)}, u32[]{:S(2)}) %collective-permute-start.52) | collective-permute-done | bytes 122912 | tf_op jit(solution)/shard_map/ppermute | solution.py:532
  255.5 4.7 %collective-permute-done.59 = bf16[120,768]{1,0:T(8,128)(2,1)S(1)} collective-permute-done((bf16[120,768]{1,0:T(8,128)(2,1)S(1)}, bf16[120,768]{1,0:T(8,128)(2,1)S(1)}, u32[]{:S(2)}, u32[]{:S(2)}) %collective-permute-start.59) | collective-permute-done | bytes 184352 | tf_op jit(solution)/shard_map/ppermute | solution.py:532
  267.7 10.8 %collective-permute-done.60 = bf16[480,768]{1,0:T(8,128)(2,1)S(1)} collective-permute-done((bf16[480,768]{1,0:T(8,128)(2,1)S(1)}, bf16[480,768]{1,0:T(8,128)(2,1)S(1)}, u32[]{:S(2)}, u32[]{:S(2)}) %collective-permute-start.60) | collective-permute-done | bytes 737312 | tf_op jit(solution)/shard_map/ppermute | solution.py:532
  (329 shorter events, 100.6 us)
Async XLA Ops:
  0.7 25.5 %collective-permute-start.2 = (bf16[3,192,768]{2,1,0:T(8,128)(2,1)}, bf16[3,192,768]{2,1,0:T(8,128)(2,1)S(1)}, u32[]{:S(2)}, u32[]{:S(2)}) collective-permute-start(bf16[3,192,768]{2,1,0:T(8,128)(2,1)} %bitcast.30), channel_id=1, source_target_pairs={{0,2},{1,3},{2,0},{3,1},{4,6},{5,7},{6,4},{7,5},{8,10},{9,11},{10,... | collective-permute-start | bytes 2654216 | tf_op jit(solution)/shard_map/ppermute | solution.py:532
  2.5 23.7 %collective-permute-start.3 = (f32[2,192]{1,0:T(2,128)}, f32[2,192]{1,0:T(2,128)S(1)}, u32[]{:S(2)}, u32[]{:S(2)}) collective-permute-start(f32[2,192]{1,0:T(2,128)} %b_one.1), channel_id=1, source_target_pairs={{0,2},{1,3},{2,0},{3,1},{4,6},{5,7},{6,4},{7,5},{8,10},{9,11},{10,... | collective-permute-start | bytes 4616 | tf_op jit(solution)/shard_map/ppermute | solution.py:532
  28.3 20.7 %collective-permute-start.8 = (bf16[192,768]{1,0:T(8,128)(2,1)S(1)}, bf16[192,768]{1,0:T(8,128)(2,1)S(1)}, u32[]{:S(2)}, u32[]{:S(2)}) collective-permute-start(bf16[192,768]{1,0:T(8,128)(2,1)S(1)} %copy-done.62), channel_id=1, source_target_pairs={{0,1},{1,0},{2,3},{3,2},{4,5},{5,4},{6,7},{7,6},{8,9},{9,8},{10,11... | collective-permute-start | bytes 884744 | tf_op jit(solution)/shard_map/ppermute | solution.py:532
  28.3 28.2 %collective-permute-start.10 = (bf16[768,768]{1,0:T(8,128)(2,1)S(1)}, bf16[768,768]{1,0:T(8,128)(2,1)S(1)}, u32[]{:S(2)}, u32[]{:S(2)}) collective-permute-start(bf16[768,768]{1,0:T(8,128)(2,1)S(1)} %copy-done), channel_id=1, source_target_pairs={{0,1},{1,0},{2,3},{3,2},{4,5},{5,4},{6,7},{7,6},{8,9},{9,8},{10,11... | collective-permute-start | bytes 3538952 | tf_op jit(solution)/shard_map/ppermute | solution.py:532
  28.8 19.6 %collective-permute-start.7 = (bf16[384,768]{1,0:T(8,128)(2,1)S(1)}, bf16[384,768]{1,0:T(8,128)(2,1)S(1)}, u32[]{:S(2)}, u32[]{:S(2)}) collective-permute-start(bf16[384,768]{1,0:T(8,128)(2,1)S(1)} %constant_dynamic-slice_fusion.19), channel_id=1, source_target_pairs={{0,2},{1,3},{2,0},{3,1},{4,6},{5,7},{6,4},{7,5},{8,10},{9,11},{10,... | collective-permute-start | bytes 1769480 | tf_op jit(solution)/shard_map/ppermute | solution.py:532
  30.2 26.3 %collective-permute-start.11 = (bf16[768,768]{1,0:T(8,128)(2,1)S(1)}, bf16[768,768]{1,0:T(8,128)(2,1)S(1)}, u32[]{:S(2)}, u32[]{:S(2)}) collective-permute-start(bf16[768,768]{1,0:T(8,128)(2,1)S(1)} %copy-done.7), channel_id=1, source_target_pairs={{0,1},{1,0},{2,3},{3,2},{4,5},{5,4},{6,7},{7,6},{8,9},{9,8},{10,11... | collective-permute-start | bytes 3538952 | tf_op jit(solution)/shard_map/ppermute | solution.py:532
  49.1 30.1 %collective-permute-start.15 = (bf16[768,768]{1,0:T(8,128)(2,1)S(1)}, bf16[768,768]{1,0:T(8,128)(2,1)}, u32[]{:S(2)}, u32[]{:S(2)}) collective-permute-start(bf16[768,768]{1,0:T(8,128)(2,1)S(1)} %copy-done.7), channel_id=1, source_target_pairs={{0,2},{1,3},{2,0},{3,1},{4,6},{5,7},{6,4},{7,5},{8,10},{9,11},{10,... | collective-permute-start | bytes 3538952 | tf_op jit(solution)/shard_map/ppermute | solution.py:532
  55.0 23.4 %collective-permute-start.13 = (bf16[384,768]{1,0:T(8,128)(2,1)S(1)}, bf16[384,768]{1,0:T(8,128)(2,1)}, u32[]{:S(2)}, u32[]{:S(2)}) collective-permute-start(bf16[384,768]{1,0:T(8,128)(2,1)S(1)} %collective-permute-done.7.refs_0_), channel_id=1, source_target_pairs={{0,4},{4,0},{8,12},{12,8},{16,20},{20,16},{24,28},{28,24},{1,5},{5... | collective-permute-start | bytes 1769480 | tf_op jit(solution)/shard_map/ppermute | solution.py:532
  56.5 21.9 %collective-permute-start.14 = (bf16[384,768]{1,0:T(8,128)(2,1)S(1)}, bf16[384,768]{1,0:T(8,128)(2,1)S(1)}, u32[]{:S(2)}, u32[]{:S(2)}) collective-permute-start(bf16[384,768]{1,0:T(8,128)(2,1)S(1)} %collective-permute-done.7.refs_0_), channel_id=1, source_target_pairs={{0,1},{1,0},{2,3},{3,2},{4,5},{5,4},{6,7},{7,6},{8,9},{9,8},{10,11... | collective-permute-start | bytes 1769480 | tf_op jit(solution)/shard_map/ppermute | solution.py:532
  83.3 26.4 %collective-permute-start.20 = (bf16[768,768]{1,0:T(8,128)(2,1)}, bf16[768,768]{1,0:T(8,128)(2,1)S(1)}, u32[]{:S(2)}, u32[]{:S(2)}) collective-permute-start(bf16[768,768]{1,0:T(8,128)(2,1)} %copy-done.12), channel_id=1, source_target_pairs={{0,1},{1,0},{2,3},{3,2},{4,5},{5,4},{6,7},{7,6},{8,9},{9,8},{10,11... | collective-permute-start | bytes 3538952 | tf_op jit(solution)/shard_map/ppermute | solution.py:532
  83.8 25.9 %collective-permute-start.21 = (bf16[768,768]{1,0:T(8,128)(2,1)}, bf16[768,768]{1,0:T(8,128)(2,1)S(1)}, u32[]{:S(2)}, u32[]{:S(2)}) collective-permute-start(bf16[768,768]{1,0:T(8,128)(2,1)} %copy-done.11), channel_id=1, source_target_pairs={{0,1},{1,0},{2,3},{3,2},{4,5},{5,4},{6,7},{7,6},{8,9},{9,8},{10,11... | collective-permute-start | bytes 3538952 | tf_op jit(solution)/shard_map/ppermute | solution.py:532
  133.4 18.1 %collective-permute-start.28 = (bf16[640,768]{1,0:T(8,128)(2,1)S(1)}, bf16[640,768]{1,0:T(8,128)(2,1)S(1)}, u32[]{:S(2)}, u32[]{:S(2)}) collective-permute-start(bf16[640,768]{1,0:T(8,128)(2,1)S(1)} %fusion.5), channel_id=1, source_target_pairs={{0,1},{1,0},{2,3},{3,2},{4,5},{5,4},{6,7},{7,6},{8,9},{9,8},{10,11... | collective-permute-start | bytes 2949128 | tf_op jit(solution)/shard_map/ppermute | solution.py:532
  136.4 21.5 %collective-permute-start.32 = (bf16[192,768]{1,0:T(8,128)(2,1)S(1)}, bf16[192,768]{1,0:T(8,128)(2,1)S(1)}, u32[]{:S(2)}, u32[]{:S(2)}) collective-permute-start(bf16[192,768]{1,0:T(8,128)(2,1)S(1)} %get-tuple-element.311), channel_id=1, source_target_pairs={{0,4},{4,0},{8,12},{12,8},{16,20},{20,16},{24,28},{28,24},{1,5},{5... | collective-permute-start | bytes 884744 | tf_op jit(solution)/shard_map/ppermute | solution.py:532
  138.3 33.0 %collective-permute-start.33 = (bf16[576,768]{1,0:T(8,128)(2,1)S(1)}, bf16[576,768]{1,0:T(8,128)(2,1)S(1)}, u32[]{:S(2)}, u32[]{:S(2)}) collective-permute-start(bf16[576,768]{1,0:T(8,128)(2,1)S(1)} %pad_maximum_fusion.4), channel_id=1, source_target_pairs={{0,2},{1,3},{2,0},{3,1},{4,6},{5,7},{6,4},{7,5},{8,10},{9,11},{10,... | collective-permute-start | bytes 2654216 | tf_op jit(solution)/shard_map/ppermute | solution.py:532
  151.9 19.5 %collective-permute-start.31 = (bf16[320,768]{1,0:T(8,128)(2,1)S(1)}, bf16[320,768]{1,0:T(8,128)(2,1)S(1)}, u32[]{:S(2)}, u32[]{:S(2)}) collective-permute-start(bf16[320,768]{1,0:T(8,128)(2,1)S(1)} %get-tuple-element.298), channel_id=1, source_target_pairs={{0,4},{4,0},{8,12},{12,8},{16,20},{20,16},{24,28},{28,24},{1,5},{5... | collective-permute-start | bytes 1474568 | tf_op jit(solution)/shard_map/ppermute | solution.py:532
  152.8 18.6 %collective-permute-start.34 = (bf16[96,768]{1,0:T(8,128)(2,1)S(1)}, bf16[96,768]{1,0:T(8,128)(2,1)S(1)}, u32[]{:S(2)}, u32[]{:S(2)}) collective-permute-start(bf16[96,768]{1,0:T(8,128)(2,1)S(1)} %get-tuple-element.309), channel_id=1, source_target_pairs={{0,8},{4,12},{8,0},{12,4},{16,24},{20,28},{24,16},{28,20},{1,9},{5... | collective-permute-start | bytes 442376 | tf_op jit(solution)/shard_map/ppermute | solution.py:532
  179.3 20.4 %collective-permute-start.38 = (bf16[320,768]{1,0:T(8,128)(2,1)S(1)}, bf16[320,768]{1,0:T(8,128)(2,1)S(1)}, u32[]{:S(2)}, u32[]{:S(2)}) collective-permute-start(bf16[320,768]{1,0:T(8,128)(2,1)S(1)} %get-tuple-element.296), channel_id=1, source_target_pairs={{0,4},{4,0},{8,12},{12,8},{16,20},{20,16},{24,28},{28,24},{1,5},{5... | collective-permute-start | bytes 1474568 | tf_op jit(solution)/shard_map/ppermute | solution.py:532
  200.6 31.8 %collective-permute-start.56 = (bf16[120,768]{1,0:T(8,128)(2,1)S(1)}, bf16[120,768]{1,0:T(8,128)(2,1)S(1)}, u32[]{:S(2)}, u32[]{:S(2)}) collective-permute-start(bf16[120,768]{1,0:T(8,128)(2,1)S(1)} %get-tuple-element.306), channel_id=1, source_target_pairs={{0,24},{4,28},{8,16},{12,20},{16,8},{20,12},{24,0},{28,4},{1,25},{... | collective-permute-start | bytes 552968 | tf_op jit(solution)/shard_map/ppermute | solution.py:532
  201.1 31.2 %collective-permute-start.55 = (bf16[120,768]{1,0:T(8,128)(2,1)S(1)}, bf16[120,768]{1,0:T(8,128)(2,1)S(1)}, u32[]{:S(2)}, u32[]{:S(2)}) collective-permute-start(bf16[120,768]{1,0:T(8,128)(2,1)S(1)} %get-tuple-element.305), channel_id=1, source_target_pairs={{0,16},{4,20},{8,24},{12,28},{16,0},{20,4},{24,8},{28,12},{1,17},{... | collective-permute-start | bytes 552968 | tf_op jit(solution)/shard_map/ppermute | solution.py:532
  228.1 33.7 %collective-permute-start.61 = (bf16[384,768]{1,0:T(8,128)(2,1)S(1)}, bf16[384,768]{1,0:T(8,128)(2,1)S(1)}, u32[]{:S(2)}, u32[]{:S(2)}) collective-permute-start(bf16[384,768]{1,0:T(8,128)(2,1)S(1)} %constant_dynamic-update-slice_fusion.5), channel_id=1, source_target_pairs={{0,4},{4,0},{8,12},{12,8},{16,20},{20,16},{24,28},{28,24},{1,5},{5... | collective-permute-start | bytes 1769480 | tf_op jit(solution)/shard_map/ppermute | solution.py:532
  232.4 21.4 %collective-permute-start.52 = (bf16[80,768]{1,0:T(8,128)(2,1)S(1)}, bf16[80,768]{1,0:T(8,128)(2,1)S(1)}, u32[]{:S(2)}, u32[]{:S(2)}) collective-permute-start(bf16[80,768]{1,0:T(8,128)(2,1)S(1)} %get-tuple-element.275), channel_id=1, source_target_pairs={{0,24},{4,28},{8,16},{12,20},{16,8},{20,12},{24,0},{28,4},{1,25},{... | collective-permute-start | bytes 368648 | tf_op jit(solution)/shard_map/ppermute | solution.py:532
  235.1 20.1 %collective-permute-start.57 = (bf16[120,768]{1,0:T(8,128)(2,1)S(1)}, bf16[120,768]{1,0:T(8,128)(2,1)S(1)}, u32[]{:S(2)}, u32[]{:S(2)}) collective-permute-start(bf16[120,768]{1,0:T(8,128)(2,1)S(1)} %get-tuple-element.273), channel_id=1, source_target_pairs={{0,8},{4,12},{8,0},{12,4},{16,24},{20,28},{24,16},{28,20},{1,9},{5... | collective-permute-start | bytes 552968 | tf_op jit(solution)/shard_map/ppermute | solution.py:532
  240.5 19.7 %collective-permute-start.59 = (bf16[120,768]{1,0:T(8,128)(2,1)S(1)}, bf16[120,768]{1,0:T(8,128)(2,1)S(1)}, u32[]{:S(2)}, u32[]{:S(2)}) collective-permute-start(bf16[120,768]{1,0:T(8,128)(2,1)S(1)} %get-tuple-element.273), channel_id=1, source_target_pairs={{0,24},{4,28},{8,16},{12,20},{16,8},{20,12},{24,0},{28,4},{1,25},{... | collective-permute-start | bytes 552968 | tf_op jit(solution)/shard_map/ppermute | solution.py:532
  260.2 18.3 %collective-permute-start.60 = (bf16[480,768]{1,0:T(8,128)(2,1)S(1)}, bf16[480,768]{1,0:T(8,128)(2,1)S(1)}, u32[]{:S(2)}, u32[]{:S(2)}) collective-permute-start(bf16[480,768]{1,0:T(8,128)(2,1)S(1)} %constant_dynamic-update-slice_fusion.9), channel_id=1, source_target_pairs={{0,4},{4,0},{8,12},{12,8},{16,20},{20,16},{24,28},{28,24},{1,5},{5... | collective-permute-start | bytes 2211848 | tf_op jit(solution)/shard_map/ppermute | solution.py:532
  (101 other events, 865.6 us)
where the time goes:
time: 282 us; the launch traced here: 281 us
  Pallas kernels  102 us (36%)
  waiting for transfers between devices  75.4 us (27%)
  starting transfers between devices  56.3 us (20%)
  local copies, waits for them, and re-layouts  35.1 us (12%)
  other arithmetic  10.3 us (4%)
    ppermute x62, waiting for transfers between devices, exchange(): return lax.ppermute(x, axis, [(i, i ^ mask) for i in range(size)])  75.4 us
    ppermute x62, starting transfers between devices, exchange(): return lax.ppermute(x, axis, [(i, i ^ mask) for i in range(size)])  56.3 us
    pallas_call x2, Pallas kernels, feed(): pl.pallas_call(functools.partial(feed_kernel, again, per), grid_spec=pltp...  35.3 us
    unnamed x133, local copies, waits for them, and re-layouts  29.8 us
    pallas_call x2, Pallas kernels, unattend(): pl.pallas_call(unattend_kernel, grid_spec=pltpu.PrefetchScalarGridSpec(nu...  23.8 us
    pallas_call x2, Pallas kernels, attend(): pl.pallas_call(functools.partial(attend_kernel, first), grid_spec=pltpu.P...  20.9 us
    pallas_call x1, Pallas kernels, project(): pl.pallas_call(project_kernel, grid=(items,), in_specs=[per_item((rows, d...  7.34 us
    pallas_call x1, Pallas kernels, unnorm(): pl.pallas_call(unnorm_kernel, grid=(items,), in_specs=[per_item((rows, wi...  6.47 us
  transfers between devices with their start and end apart: 62, of which 23 were waited for; matrix products, arithmetic and copies ran while one was open for 6% of the time, Pallas kernels for 36%

commit v1 on v0

--- a/solution.py
+++ b/solution.py
@@ -11,7 +11,8 @@
 WORDS = 40
 PACK = 16
 LANES = 128
-BLOCK = 256
+BLOCK = 768
+CHUNK = 256
 
 norm_eps = 1e-06
 masked_value = -1000000000.0
@@ -78,6 +79,14 @@
 
 def lasting(us):
     return pl.CostEstimate(flops=int(us * 1.15e9), bytes_accessed=0, transcendentals=0)
+
+
+def later(shape, dtype):
+    return pltpu.HBM(shape, dtype)
+
+
+def in_hbm(x):
+    return pltpu.with_memory_space_constraint(x, pltpu.HBM)
 
 
 def params(mib):
@@ -200,7 +209,7 @@
 ):
     n_weights = 6 if again else 4
     weights, rest = refs[:n_weights], refs[n_weights:]
-    bias_a, bias_b, grad_ref, hidden_ref, dup_a, dup_b, ddown_a, ddown_b, dbias_ref, gu_ref = rest
+    bias_a, bias_b, grad_ref, hidden_ref, dup_a, dup_b, ddown_a, ddown_b, dbias_ref, gu_ref, ddown_all, dup_all = rest
     step = pl.program_id(0)
     items, rows, dim = normed.shape
     is_a = step < per
@@ -222,8 +231,7 @@
         w_up = jnp.where(is_a, up_a[...], up_c[...])
     w_down = jnp.where(is_a, down_a[...], down_c[...])
     bias = jnp.where(is_a, bias_a[...].astype(f32), bias_b[...].astype(f32))
-    bias_sum = jnp.zeros((1, w_up.shape[1]), f32)
-    for i in range(items):
+    def one_item(i, bias_sum):
         up = mul_nn(normed[i], w_up) + bias
         grad_hidden = mul_nt(cot[i], w_down)
         cdf = 0.5 * (1.0 + lax.erf(up * 0.7071067811865476))
@@ -231,24 +239,33 @@
         gu = (slope * grad_hidden).astype(bf)
         hidden_ref[i] = (up * cdf).astype(bf)
         gu_ref[i] = gu
-        bias_sum = bias_sum + col_sum(gu.astype(f32))
         grad_ref[i] += mul_nt(gu, w_up)
+        return bias_sum + col_sum(gu.astype(f32))
+
+    bias_sum = lax.fori_loop(
+        0, items, one_item, jnp.zeros((1, w_up.shape[1]), f32), unroll=bool(again)
+    )
     dbias_ref[...] = bias_sum
-    flat = (items * rows, dim)
-    hidden = hidden_ref[...].reshape(items * rows, -1)
-    gu = gu_ref[...].reshape(items * rows, -1)
-    ddown = mul_tn(hidden, cot[...].reshape(flat)).astype(bf)
-    dup = mul_tn(normed[...].reshape(flat), gu).astype(bf)
+    flat = items * rows
+
+    def rows_of(n, carry):
+        at = pl.ds(pl.multiple_of(n * CHUNK, CHUNK), CHUNK)
+        take = lambda ref: ref[:, :, at].reshape(flat, CHUNK)
+        ddown_all[at, :] = mul_tn(take(hidden_ref), cot[...].reshape(flat, dim)).astype(bf)
+        dup_all[at, :] = mul_tn(take(normed), gu_ref[...].reshape(flat, -1)).astype(bf)
+        return carry
+
+    lax.fori_loop(0, dim // CHUNK, rows_of, 0)
 
     @pl.when(is_a)
     def _():
-        ddown_a[...] = ddown
-        dup_a[...] = dup
+        ddown_a[...] = ddown_all[...]
+        dup_a[...] = dup_all[...]
 
     @pl.when(jnp.logical_not(is_a))
     def _():
-        ddown_b[...] = ddown
-        dup_b[...] = dup
+        ddown_b[...] = ddown_all[...]
+        dup_b[...] = dup_all[...]
 
 
 def feed(low_half, normed, cot, base_grad, ups, downs, biases):
@@ -284,21 +301,21 @@
                 down(second),
                 pl.BlockSpec((1, BLOCK), lambda j, *_: (0, j)),
             ],
-            scratch_shapes=[pltpu.VMEM((items, rows, BLOCK), bf)],
+            scratch_shapes=[pltpu.VMEM((items, rows, BLOCK), bf)] + [pltpu.VMEM((dim, dim), bf)] * 2,
         ),
         out_shape=[
             jax.ShapeDtypeStruct((items, rows, dim), f32),
-            jax.ShapeDtypeStruct((items, rows, 2 * units), bf),
+            later((items, rows, 2 * units), bf),
             jax.ShapeDtypeStruct((dim, units), bf),
             jax.ShapeDtypeStruct((dim, units), bf),
             jax.ShapeDtypeStruct((units, dim), bf),
             jax.ShapeDtypeStruct((units, dim), bf),
             jax.ShapeDtypeStruct((1, 2 * units), f32),
         ],
-        compiler_params=params(14),
+        compiler_params=params(36 if again else 24),
         cost_estimate=lasting(TIMES["feed"]),
         name="feed",
-    )(low_half, normed, cot, base_grad, *ups, *downs, *biases)
+    )(low_half, *(map(in_hbm, (normed, cot, base_grad, *ups, *downs)) if again else (normed, cot, base_grad, *ups, *downs)), *biases)
 
 
 def project_kernel(middle, small, hidden_a, hidden_b, *refs):
@@ -434,11 +451,14 @@
         items, _, dim = normed.shape
         flat = normed[...].reshape(items * rows, dim)
         quarter = width // 2
-        for c in range(3):
-            g = g_ref[:, :, c * width : (c + 1) * width].reshape(items * rows, width)
-            dw = mul_tn(g, flat).astype(bf)
+        def one_kind(c, carry):
+            at = pl.ds(pl.multiple_of(c * width, LANES), width)
+            dw = mul_tn(g_ref[:, :, at].reshape(items * rows, width), flat).astype(bf)
             dw_out[0, c] = dw[:quarter]
             dw_out[1, c] = dw[quarter:]
+            return carry
+
+        lax.fori_loop(0, 3, one_kind, 0)
 
 
 def unattend(counts, q, k, v, gmix, logs, normed):
@@ -657,7 +677,8 @@
     q_b, k_b, v_b, mixed_b, log_b = attend(
         False, counts, tokens3, vectors, w_b, [b_peer, mate(b_peer)], rows
     )
-    mixed_b, out_peer, up_first, down_later = tie(mixed_b, out_peer, up_first, w_down)
+    mixed_b, out_peer, up_first, bias_peer, down_later = tie(mixed_b, out_peer, up_first, bias_peer, w_down)
+    bias_far = mate(bias_peer)
     down_peer = peer(down_later)
     out_a = jnp.concatenate([w_out, out_mate], axis=0)
     out_b = jnp.concatenate([out_peer, mate(out_peer)], axis=0)
@@ -680,7 +701,7 @@
     ups = [up_first, up_second, up_first_far, up_second_far]
     downs = [down_peer, mate(down_peer)]
     grad_norm2, hidden_b, dup_peer, dup_far, ddown_peer, ddown_far, dbias_b = feed(
-        flag, normed2, cot_pad, grad_part, ups, downs, [bias_peer, mate(bias_peer)]
+        flag, normed2, cot_pad, grad_part, ups, downs, [bias_peer, bias_far]
     )
     grad_norm2, dup_peer, dup_far, ddown_peer, ddown_far, got_up, got_down = tie(
         grad_norm2, dup_peer, dup_far, ddown_peer, ddown_far, got_up, got_down

time: 282 us -> 275 us (0.975)
  local copies, waits for them, and re-layouts: 35.1 us -> 24.6 us
    unnamed x133 -> x123, local copies, waits for them, and re-layouts: 29.8 us -> 19.3 us
  transfers between devices with their start and end apart: 62 -> 62, of which waited for: 23 -> 25; matrix products, arithmetic and copies ran while one was open for 6% -> 6% of each run, Pallas kernels for 36% -> 38%
where the time goes in v1:
time: 275 us
  Pallas kernels  104 us (38%)
  waiting for transfers between devices  75.9 us (28%)
  starting transfers between devices  58.5 us (21%)
  local copies, waits for them, and re-layouts  24.6 us (9%)
  other arithmetic  10.2 us (4%)
    ppermute x62, waiting for transfers between devices, exchange(): return lax.ppermute(x, axis, [(i, i ^ mask) for i in range(size)])  75.9 us
    ppermute x62, starting transfers between devices, exchange(): return lax.ppermute(x, axis, [(i, i ^ mask) for i in range(size)])  58.5 us
    pallas_call x2, Pallas kernels, feed(): pl.pallas_call(functools.partial(feed_kernel, again, per), grid_spec=pltp...  35.8 us
    pallas_call x2, Pallas kernels, unattend(): pl.pallas_call(unattend_kernel, grid_spec=pltpu.PrefetchScalarGridSpec(nu...  24.9 us
    pallas_call x2, Pallas kernels, attend(): pl.pallas_call(functools.partial(attend_kernel, first), grid_spec=pltpu.P...  20.9 us
    unnamed x123, local copies, waits for them, and re-layouts  19.3 us
    pallas_call x1, Pallas kernels, project(): pl.pallas_call(project_kernel, grid=(items,), in_specs=[per_item((rows, d...  7.25 us
    pallas_call x1, Pallas kernels, unnorm(): pl.pallas_call(unnorm_kernel, grid=(items,), in_specs=[per_item((rows, wi...  6.5 us
  transfers between devices with their start and end apart: 62, of which 25 were waited for; matrix products, arithmetic and copies ran while one was open for 6% of the time, Pallas kernels for 38%

profile of v1, /device:TPU:8, one launch (start us, length us, event | category | flops | bytes accessed | tf_op | source)
XLA Modules:
  0.0 274.5 jit_solution(7902977599888036529)
XLA Ops:
  11.4 10.5 %attend.2 = (bf16[3,288,384]{2,1,0:T(8,128)(2,1)S(1)}, bf16[3,288,384]{2,1,0:T(8,128)(2,1)S(1)}, bf16[3,288,384]{2,1,0:T(8,128)(2,1)S(1)}, bf16[3,288,384]{2,1,0...) custom-call(s32[3]{0:T(128)S(1)} %dynamic_slice.78.counts, ...), custom_call_target="tpu_custom_call" | custom-call | flops 11500000256 | tf_op jit(solution)/shard_map/attend/pallas_call | solution.py:150
  31.4 10.4 %attend.3 = (bf16[3,288,384]{2,1,0:T(8,128)(2,1)S(1)}, bf16[3,288,384]{2,1,0:T(8,128)(2,1)S(1)}, bf16[3,288,384]{2,1,0:T(8,128)(2,1)S(1)}, bf16[3,288,384]{2,1,0:T(8,128)(2,1)S(1)}, f32[3,8,288]{2,1,0:T(8,128)S(1)}) custom-call(s32[3]{0:T(128)S(1)} %dynamic_slice.78.counts, bf16[3,280,768]{2,1,0:T(8,128)(2,1)S(1)} %bitcast.26, ...), custom_call_target="tpu_custom_call" | custom-call | flops 11500000256 | tf_op jit(solution)/shard_map/attend/pallas_call | solution.py:150
  44.2 4.9 %collective-permute-done.7.refs_0_ = bf16[384,768]{1,0:T(8,128)(2,1)S(1)} collective-permute-done((bf16[384,768]{1,0:T(8,128)(2,1)S(1)}, bf16[384,768]{1,0:T(8,128)(2,1)S(1)}, u32[]{:S(2)}, u32[]{:S(2)}) %collective-permute-start.7) | collective-permute-done | bytes 589856 | tf_op jit(solution)/shard_map/ppermute | solution.py:552
  50.7 2.7 branch.1
  56.5 16.4 %feed.2 = (f32[3,288,768]{2,1,0:T(8,128)S(1)}, bf16[3,288,1536]{2,1,0:T(8,128)(2,1)}, bf16[768,768]{1,0:T(8,128)(2,1)S(1)}, bf16[768,768]{1,0:T(8,128)(2,1)S(1)}...) custom-call(s32[1]{0:T(128)} %bitcast.3.low_half, ...), custom_call_target="tpu_custom_call" | custom-call | flops 20700000256 | tf_op jit(solution)/shard_map/feed/pallas_call | solution.py:285
  82.6 19.4 %feed.3 = (f32[3,288,768]{2,1,0:T(8,128)S(1)}, bf16[3,288,1536]{2,1,0:T(8,128)(2,1)}, bf16[768,768]{1,0:T(8,128)(2,1)S(1)}, bf16[768,768]{1,0:T(8,128)(2,1)S(1)}...) custom-call(s32[1]{0:T(128)} %bitcast.3.low_half, ...), custom_call_target="tpu_custom_call" | custom-call | flops 20700000256 | tf_op jit(solution)/shard_map/feed/pallas_call | solution.py:285
  102.7 5.9 %unbranch.1 = (f32[3,288,768]{2,1,0:T(8,128)S(1)}, bf16[3,288,384]{2,1,0:T(8,128)(2,1)S(1)}, bf16[3,288,384]{2,1,0:T(8,128)(2,1)S(1)}, bf16[4,192,768]{2,1,0:T(8,128)(2,1)S(1)}, f32[8,768]{1,0:T(8,128)S(1)}) custom-call(f32[3,288,768]{2,1,0:T(8,128)S(1)} %copy-done.26, bf16[3,288,768]{2,1,0:T(8,128)(2,1)S(1)} %copy-done.30, ...), custom_call_target="tpu_custom_call" | custom-call | flops 6899999744 | tf_op jit(solution)/shard_map/unbranch/pallas_call | solution.py:386
  112.1 12.4 %unattend.2 = (bf16[3,288,1152]{2,1,0:T(8,128)(2,1)S(1)}, bf16[2,3,192,768]{3,2,1,0:T(8,128)(2,1)S(1)}, f32[8,384]{1,0:T(8,128)S(1)}) custom-call(s32[3]{0:T(128)S(1)} %copy-done.24, bf16[3,288,384]{2,1,0:T(8,128)(2,1)S(1)} %copy-done.46, bf16[3,288,384]{2,1,0:T(8,128)(2,1)S(1)} %copy-done.48, bf16[3,288,384]{2,1,0:T(8,128)(2,1)S(1)} %copy-done.50, ...), custom_call_target="tpu_custom_call" | custom-call | flops 12650000384 | tf_op jit(solution)/shard_map/unattend/pallas_call | solution.py:467
  132.7 7.3 %project.1 = f32[3,280,768]{2,1,0:T(8,128)} custom-call(f32[3,288,768]{2,1,0:T(8,128)S(1)} %copy-done.26, f32[6,768]{1,0:T(8,128)S(1)} %copy-done.2, bf16[3,288,1536]{2,1,0:T(8,128)(2,1)S(1)} %copy-done.27, bf16[3,288,1536]{2,1,0:T(8,128)(2,1)S(1)} %copy-done.28, bf16[768,768]{1,0:T(8,128)(2,1)S(1)} %copy-done.8, bf16[768,768]{1,0:T(8,128)(2,1)S(1)} %copy-done.10, ...), custom_call_target="tpu_custom_call" | custom-call | flops 6899999744 | tf_op jit(solution)/shard_map/project/pallas_call | solution.py:334
  146.5 2.6 collective-permute-start.35
  151.7 12.4 %unattend.3 = (bf16[3,288,1152]{2,1,0:T(8,128)(2,1)S(1)}, bf16[2,3,192,768]{3,2,1,0:T(8,128)(2,1)S(1)}, f32[8,384]{1,0:T(8,128)S(1)}) custom-call(s32[3]{0:T(128)S(1)} %copy-done.24, bf16[3,288,384]{2,1,0:T(8,128)(2,1)S(1)} %copy-done.40, bf16[3,288,384]{2,1,0:T(8,128)(2,1)S(1)} %copy-done.42, bf16[3,288,384]{2,1,0:T(8,128)(2,1)S(1)} %copy-done.44, ...), custom_call_target="tpu_custom_call" | custom-call | flops 12650000384 | tf_op jit(solution)/shard_map/unattend/pallas_call | solution.py:467
  173.8 6.5 %unnorm.1 = (f32[3,280,768]{2,1,0:T(8,128)}, f32[8,768]{1,0:T(8,128)S(1)}) custom-call(bf16[3,288,1152]{2,1,0:T(8,128)(2,1)S(1)} %get-tuple-element.240.g_a, bf16[3,288,1152]{2,1,0:T(8,128)(2,1)S(1)} %get-tuple-element.241.g_b, bf16[3,192,768]{2,1,0:T(8,128)(2,1)S(1)} %bitcast.32, bf16[3,192,768]{2,1,0:T(8,128)(2,1)S(1)} %copy-done.16, ...), custom_call_target="tpu_custom_call" | custom-call | flops 6899999744 | tf_op jit(solution)/shard_map/unnorm/pallas_call | solution.py:510
  183.5 9.2 %collective-permute-done.38 = bf16[320,768]{1,0:T(8,128)(2,1)S(1)} collective-permute-done((bf16[320,768]{1,0:T(8,128)(2,1)S(1)}, bf16[320,768]{1,0:T(8,128)(2,1)S(1)}, u32[]{:S(2)}, u32[]{:S(2)}) %collective-permute-start.38) | collective-permute-done | bytes 491552 | tf_op jit(solution)/shard_map/ppermute | solution.py:552
  194.1 4.4 %collective-permute-start.55 = (bf16[120,768]{1,0:T(8,128)(2,1)S(1)}, bf16[120,768]{1,0:T(8,128)(2,1)S(1)}, u32[]{:S(2)}, u32[]{:S(2)}) collective-permute-start(bf16[120,768]{1,0:T(8,128)(2,1)S(1)} %get-tuple-element.307), channel_id=1, source_target_pairs={{0,16},{4,20},{8,24},{12,28},{16,0},{20,4},{24,8},{28,12},{1,17},{... | collective-permute-start | bytes 552968 | tf_op jit(solution)/shard_map/ppermute | solution.py:552
  199.7 2.5 collective-permute-done.45
  203.2 2.6 collective-permute-done.46
  207.2 2.6 collective-permute-start.47
  209.8 11.0 %collective-permute-done.49 = bf16[80,768]{1,0:T(8,128)(2,1)S(1)} collective-permute-done((bf16[80,768]{1,0:T(8,128)(2,1)S(1)}, bf16[80,768]{1,0:T(8,128)(2,1)S(1)}, u32[]{:S(2)}, u32[]{:S(2)}) %collective-permute-start.49) | collective-permute-done | bytes 122912 | tf_op jit(solution)/shard_map/ppermute | solution.py:552
  222.1 3.6 %collective-permute-start.50 = (bf16[80,768]{1,0:T(8,128)(2,1)S(1)}, bf16[80,768]{1,0:T(8,128)(2,1)S(1)}, u32[]{:S(2)}, u32[]{:S(2)}) collective-permute-start(bf16[80,768]{1,0:T(8,128)(2,1)S(1)} %get-tuple-element.277), channel_id=1, source_target_pairs={{0,8},{4,12},{8,0},{12,4},{16,24},{20,28},{24,16},{28,20},{1,9},{5... | collective-permute-start | bytes 368648 | tf_op jit(solution)/shard_map/ppermute | solution.py:552
  227.6 2.9 %collective-permute-start.57 = (bf16[120,768]{1,0:T(8,128)(2,1)S(1)}, bf16[120,768]{1,0:T(8,128)(2,1)S(1)}, u32[]{:S(2)}, u32[]{:S(2)}) collective-permute-start(bf16[120,768]{1,0:T(8,128)(2,1)S(1)} %get-tuple-element.275), channel_id=1, source_target_pairs={{0,8},{4,12},{8,0},{12,4},{16,24},{20,28},{24,16},{28,20},{1,9},{5... | collective-permute-start | bytes 552968 | tf_op jit(solution)/shard_map/ppermute | solution.py:552
  230.9 2.6 collective-permute-start.58
  236.2 11.0 %collective-permute-done.52 = bf16[80,768]{1,0:T(8,128)(2,1)S(1)} collective-permute-done((bf16[80,768]{1,0:T(8,128)(2,1)S(1)}, bf16[80,768]{1,0:T(8,128)(2,1)S(1)}, u32[]{:S(2)}, u32[]{:S(2)}) %collective-permute-start.52) | collective-permute-done | bytes 122912 | tf_op jit(solution)/shard_map/ppermute | solution.py:552
  249.4 4.2 %collective-permute-done.59 = bf16[120,768]{1,0:T(8,128)(2,1)S(1)} collective-permute-done((bf16[120,768]{1,0:T(8,128)(2,1)S(1)}, bf16[120,768]{1,0:T(8,128)(2,1)S(1)}, u32[]{:S(2)}, u32[]{:S(2)}) %collective-permute-start.59) | collective-permute-done | bytes 184352 | tf_op jit(solution)/shard_map/ppermute | solution.py:552
  261.1 10.8 %collective-permute-done.60 = bf16[480,768]{1,0:T(8,128)(2,1)S(1)} collective-permute-done((bf16[480,768]{1,0:T(8,128)(2,1)S(1)}, bf16[480,768]{1,0:T(8,128)(2,1)S(1)}, u32[]{:S(2)}, u32[]{:S(2)}) %collective-permute-start.60) | collective-permute-done | bytes 737312 | tf_op jit(solution)/shard_map/ppermute | solution.py:552
  (319 shorter events, 94.2 us)
Async XLA Ops:
  0.7 24.9 %collective-permute-start.2 = (bf16[3,192,768]{2,1,0:T(8,128)(2,1)}, bf16[3,192,768]{2,1,0:T(8,128)(2,1)S(1)}, u32[]{:S(2)}, u32[]{:S(2)}) collective-permute-start(bf16[3,192,768]{2,1,0:T(8,128)(2,1)} %bitcast.30), channel_id=1, source_target_pairs={{0,2},{1,3},{2,0},{3,1},{4,6},{5,7},{6,4},{7,5},{8,10},{9,11},{10,... | collective-permute-start | bytes 2654216 | tf_op jit(solution)/shard_map/ppermute | solution.py:552
  2.5 23.1 %collective-permute-start.3 = (f32[2,192]{1,0:T(2,128)}, f32[2,192]{1,0:T(2,128)S(1)}, u32[]{:S(2)}, u32[]{:S(2)}) collective-permute-start(f32[2,192]{1,0:T(2,128)} %b_one.1), channel_id=1, source_target_pairs={{0,2},{1,3},{2,0},{3,1},{4,6},{5,7},{6,4},{7,5},{8,10},{9,11},{10,... | collective-permute-start | bytes 4616 | tf_op jit(solution)/shard_map/ppermute | solution.py:552
  28.2 21.4 %collective-permute-start.9 = (bf16[192,768]{1,0:T(8,128)(2,1)S(1)}, bf16[192,768]{1,0:T(8,128)(2,1)S(1)}, u32[]{:S(2)}, u32[]{:S(2)}) collective-permute-start(bf16[192,768]{1,0:T(8,128)(2,1)S(1)} %copy-done.55), channel_id=1, source_target_pairs={{0,1},{1,0},{2,3},{3,2},{4,5},{5,4},{6,7},{7,6},{8,9},{9,8},{10,11... | collective-permute-start | bytes 884744 | tf_op jit(solution)/shard_map/ppermute | solution.py:552
  28.2 28.2 %collective-permute-start.11 = (bf16[768,768]{1,0:T(8,128)(2,1)S(1)}, bf16[768,768]{1,0:T(8,128)(2,1)S(1)}, u32[]{:S(2)}, u32[]{:S(2)}) collective-permute-start(bf16[768,768]{1,0:T(8,128)(2,1)S(1)} %copy-done), channel_id=1, source_target_pairs={{0,1},{1,0},{2,3},{3,2},{4,5},{5,4},{6,7},{7,6},{8,9},{9,8},{10,11... | collective-permute-start | bytes 3538952 | tf_op jit(solution)/shard_map/ppermute | solution.py:552
  29.8 19.3 %collective-permute-start.7 = (bf16[384,768]{1,0:T(8,128)(2,1)S(1)}, bf16[384,768]{1,0:T(8,128)(2,1)S(1)}, u32[]{:S(2)}, u32[]{:S(2)}) collective-permute-start(bf16[384,768]{1,0:T(8,128)(2,1)S(1)} %constant_dynamic-slice_fusion.19), channel_id=1, source_target_pairs={{0,2},{1,3},{2,0},{3,1},{4,6},{5,7},{6,4},{7,5},{8,10},{9,11},{10,... | collective-permute-start | bytes 1769480 | tf_op jit(solution)/shard_map/ppermute | solution.py:552
  31.3 25.1 %collective-permute-start.12 = (bf16[768,768]{1,0:T(8,128)(2,1)S(1)}, bf16[768,768]{1,0:T(8,128)(2,1)S(1)}, u32[]{:S(2)}, u32[]{:S(2)}) collective-permute-start(bf16[768,768]{1,0:T(8,128)(2,1)S(1)} %copy-done.7), channel_id=1, source_target_pairs={{0,1},{1,0},{2,3},{3,2},{4,5},{5,4},{6,7},{7,6},{8,9},{9,8},{10,11... | collective-permute-start | bytes 3538952 | tf_op jit(solution)/shard_map/ppermute | solution.py:552
  49.7 28.1 %collective-permute-start.16 = (bf16[768,768]{1,0:T(8,128)(2,1)S(1)}, bf16[768,768]{1,0:T(8,128)(2,1)}, u32[]{:S(2)}, u32[]{:S(2)}) collective-permute-start(bf16[768,768]{1,0:T(8,128)(2,1)S(1)} %copy-done.7), channel_id=1, source_target_pairs={{0,2},{1,3},{2,0},{3,1},{4,6},{5,7},{6,4},{7,5},{8,10},{9,11},{10,... | collective-permute-start | bytes 3538952 | tf_op jit(solution)/shard_map/ppermute | solution.py:552
  54.9 21.5 %collective-permute-start.14 = (bf16[384,768]{1,0:T(8,128)(2,1)S(1)}, bf16[384,768]{1,0:T(8,128)(2,1)}, u32[]{:S(2)}, u32[]{:S(2)}) collective-permute-start(bf16[384,768]{1,0:T(8,128)(2,1)S(1)} %collective-permute-done.7.refs_0_), channel_id=1, source_target_pairs={{0,4},{4,0},{8,12},{12,8},{16,20},{20,16},{24,28},{28,24},{1,5},{5... | collective-permute-start | bytes 1769480 | tf_op jit(solution)/shard_map/ppermute | solution.py:552
  56.4 20.0 %collective-permute-start.15 = (bf16[384,768]{1,0:T(8,128)(2,1)S(1)}, bf16[384,768]{1,0:T(8,128)(2,1)S(1)}, u32[]{:S(2)}, u32[]{:S(2)}) collective-permute-start(bf16[384,768]{1,0:T(8,128)(2,1)S(1)} %collective-permute-done.7.refs_0_), channel_id=1, source_target_pairs={{0,1},{1,0},{2,3},{3,2},{4,5},{5,4},{6,7},{7,6},{8,9},{9,8},{10,11... | collective-permute-start | bytes 1769480 | tf_op jit(solution)/shard_map/ppermute | solution.py:552
  78.3 23.7 %collective-permute-start.20 = (bf16[768,768]{1,0:T(8,128)(2,1)}, bf16[768,768]{1,0:T(8,128)(2,1)S(1)}, u32[]{:S(2)}, u32[]{:S(2)}) collective-permute-start(bf16[768,768]{1,0:T(8,128)(2,1)} %copy-done.12), channel_id=1, source_target_pairs={{0,1},{1,0},{2,3},{3,2},{4,5},{5,4},{6,7},{7,6},{8,9},{9,8},{10,11... | collective-permute-start | bytes 3538952 | tf_op jit(solution)/shard_map/ppermute | solution.py:552
  78.9 23.2 %collective-permute-start.21 = (bf16[768,768]{1,0:T(8,128)(2,1)}, bf16[768,768]{1,0:T(8,128)(2,1)S(1)}, u32[]{:S(2)}, u32[]{:S(2)}) collective-permute-start(bf16[768,768]{1,0:T(8,128)(2,1)} %copy-done.11), channel_id=1, source_target_pairs={{0,1},{1,0},{2,3},{3,2},{4,5},{5,4},{6,7},{7,6},{8,9},{9,8},{10,11... | collective-permute-start | bytes 3538952 | tf_op jit(solution)/shard_map/ppermute | solution.py:552
  129.6 20.5 %collective-permute-start.32 = (bf16[192,768]{1,0:T(8,128)(2,1)S(1)}, bf16[192,768]{1,0:T(8,128)(2,1)S(1)}, u32[]{:S(2)}, u32[]{:S(2)}) collective-permute-start(bf16[192,768]{1,0:T(8,128)(2,1)S(1)} %get-tuple-element.313), channel_id=1, source_target_pairs={{0,4},{4,0},{8,12},{12,8},{16,20},{20,16},{24,28},{28,24},{1,5},{5... | collective-permute-start | bytes 884744 | tf_op jit(solution)/shard_map/ppermute | solution.py:552
  130.6 33.5 %collective-permute-start.33 = (bf16[576,768]{1,0:T(8,128)(2,1)S(1)}, bf16[576,768]{1,0:T(8,128)(2,1)S(1)}, u32[]{:S(2)}, u32[]{:S(2)}) collective-permute-start(bf16[576,768]{1,0:T(8,128)(2,1)S(1)} %pad_maximum_fusion.4), channel_id=1, source_target_pairs={{0,2},{1,3},{2,0},{3,1},{4,6},{5,7},{6,4},{7,5},{8,10},{9,11},{10,... | collective-permute-start | bytes 2654216 | tf_op jit(solution)/shard_map/ppermute | solution.py:552
  144.2 20.0 %collective-permute-start.31 = (bf16[320,768]{1,0:T(8,128)(2,1)S(1)}, bf16[320,768]{1,0:T(8,128)(2,1)S(1)}, u32[]{:S(2)}, u32[]{:S(2)}) collective-permute-start(bf16[320,768]{1,0:T(8,128)(2,1)S(1)} %get-tuple-element.300), channel_id=1, source_target_pairs={{0,4},{4,0},{8,12},{12,8},{16,20},{20,16},{24,28},{28,24},{1,5},{5... | collective-permute-start | bytes 1474568 | tf_op jit(solution)/shard_map/ppermute | solution.py:552
  146.0 18.2 %collective-permute-start.34 = (bf16[96,768]{1,0:T(8,128)(2,1)S(1)}, bf16[96,768]{1,0:T(8,128)(2,1)S(1)}, u32[]{:S(2)}, u32[]{:S(2)}) collective-permute-start(bf16[96,768]{1,0:T(8,128)(2,1)S(1)} %get-tuple-element.311), channel_id=1, source_target_pairs={{0,8},{4,12},{8,0},{12,4},{16,24},{20,28},{24,16},{28,20},{1,9},{5... | collective-permute-start | bytes 442376 | tf_op jit(solution)/shard_map/ppermute | solution.py:552
  172.1 20.5 %collective-permute-start.38 = (bf16[320,768]{1,0:T(8,128)(2,1)S(1)}, bf16[320,768]{1,0:T(8,128)(2,1)S(1)}, u32[]{:S(2)}, u32[]{:S(2)}) collective-permute-start(bf16[320,768]{1,0:T(8,128)(2,1)S(1)} %get-tuple-element.298), channel_id=1, source_target_pairs={{0,4},{4,0},{8,12},{12,8},{16,20},{20,16},{24,28},{28,24},{1,5},{5... | collective-permute-start | bytes 1474568 | tf_op jit(solution)/shard_map/ppermute | solution.py:552
  193.5 32.3 %collective-permute-start.56 = (bf16[120,768]{1,0:T(8,128)(2,1)S(1)}, bf16[120,768]{1,0:T(8,128)(2,1)S(1)}, u32[]{:S(2)}, u32[]{:S(2)}) collective-permute-start(bf16[120,768]{1,0:T(8,128)(2,1)S(1)} %get-tuple-element.308), channel_id=1, source_target_pairs={{0,24},{4,28},{8,16},{12,20},{16,8},{20,12},{24,0},{28,4},{1,25},{... | collective-permute-start | bytes 552968 | tf_op jit(solution)/shard_map/ppermute | solution.py:552
  194.1 31.7 %collective-permute-start.55 = (bf16[120,768]{1,0:T(8,128)(2,1)S(1)}, bf16[120,768]{1,0:T(8,128)(2,1)S(1)}, u32[]{:S(2)}, u32[]{:S(2)}) collective-permute-start(bf16[120,768]{1,0:T(8,128)(2,1)S(1)} %get-tuple-element.307), channel_id=1, source_target_pairs={{0,16},{4,20},{8,24},{12,28},{16,0},{20,4},{24,8},{28,12},{1,17},{... | collective-permute-start | bytes 552968 | tf_op jit(solution)/shard_map/ppermute | solution.py:552
  221.0 33.7 %collective-permute-start.61 = (bf16[384,768]{1,0:T(8,128)(2,1)S(1)}, bf16[384,768]{1,0:T(8,128)(2,1)S(1)}, u32[]{:S(2)}, u32[]{:S(2)}) collective-permute-start(bf16[384,768]{1,0:T(8,128)(2,1)S(1)} %constant_dynamic-update-slice_fusion.5), channel_id=1, source_target_pairs={{0,4},{4,0},{8,12},{12,8},{16,20},{20,16},{24,28},{28,24},{1,5},{5... | collective-permute-start | bytes 1769480 | tf_op jit(solution)/shard_map/ppermute | solution.py:552
  225.8 21.4 %collective-permute-start.52 = (bf16[80,768]{1,0:T(8,128)(2,1)S(1)}, bf16[80,768]{1,0:T(8,128)(2,1)S(1)}, u32[]{:S(2)}, u32[]{:S(2)}) collective-permute-start(bf16[80,768]{1,0:T(8,128)(2,1)S(1)} %get-tuple-element.277), channel_id=1, source_target_pairs={{0,24},{4,28},{8,16},{12,20},{16,8},{20,12},{24,0},{28,4},{1,25},{... | collective-permute-start | bytes 368648 | tf_op jit(solution)/shard_map/ppermute | solution.py:552
  227.6 20.7 %collective-permute-start.57 = (bf16[120,768]{1,0:T(8,128)(2,1)S(1)}, bf16[120,768]{1,0:T(8,128)(2,1)S(1)}, u32[]{:S(2)}, u32[]{:S(2)}) collective-permute-start(bf16[120,768]{1,0:T(8,128)(2,1)S(1)} %get-tuple-element.275), channel_id=1, source_target_pairs={{0,8},{4,12},{8,0},{12,4},{16,24},{20,28},{24,16},{28,20},{1,9},{5... | collective-permute-start | bytes 552968 | tf_op jit(solution)/shard_map/ppermute | solution.py:552
  230.9 18.5 %collective-permute-start.58 = (bf16[120,768]{1,0:T(8,128)(2,1)S(1)}, bf16[120,768]{1,0:T(8,128)(2,1)S(1)}, u32[]{:S(2)}, u32[]{:S(2)}) collective-permute-start(bf16[120,768]{1,0:T(8,128)(2,1)S(1)} %get-tuple-element.275), channel_id=1, source_target_pairs={{0,16},{4,20},{8,24},{12,28},{16,0},{20,4},{24,8},{28,12},{1,17},{... | collective-permute-start | bytes 552968 | tf_op jit(solution)/shard_map/ppermute | solution.py:552
  234.7 18.9 %collective-permute-start.59 = (bf16[120,768]{1,0:T(8,128)(2,1)S(1)}, bf16[120,768]{1,0:T(8,128)(2,1)S(1)}, u32[]{:S(2)}, u32[]{:S(2)}) collective-permute-start(bf16[120,768]{1,0:T(8,128)(2,1)S(1)} %get-tuple-element.275), channel_id=1, source_target_pairs={{0,24},{4,28},{8,16},{12,20},{16,8},{20,12},{24,0},{28,4},{1,25},{... | collective-permute-start | bytes 552968 | tf_op jit(solution)/shard_map/ppermute | solution.py:552
  253.6 18.3 %collective-permute-start.60 = (bf16[480,768]{1,0:T(8,128)(2,1)S(1)}, bf16[480,768]{1,0:T(8,128)(2,1)S(1)}, u32[]{:S(2)}, u32[]{:S(2)}) collective-permute-start(bf16[480,768]{1,0:T(8,128)(2,1)S(1)} %constant_dynamic-update-slice_fusion.9), channel_id=1, source_target_pairs={{0,4},{4,0},{8,12},{12,8},{16,20},{20,16},{24,28},{28,24},{1,5},{5... | collective-permute-start | bytes 2211848 | tf_op jit(solution)/shard_map/ppermute | solution.py:552
  (96 other events, 894.8 us)

commit v2 on v1

--- a/solution.py
+++ b/solution.py
@@ -67,13 +67,13 @@
 
 
 TIMES = {
-    "attend": 10,
-    "branch": 3,
-    "feed": 18,
-    "project": 6,
-    "unbranch": 6,
-    "unattend": 11,
-    "unnorm": 6,
+    "attend": 30,
+    "branch": 0.01,
+    "feed": 54,
+    "project": 18,
+    "unbranch": 18,
+    "unattend": 33,
+    "unnorm": 18,
 }
 
 
@@ -141,11 +141,13 @@
 def attend(first, counts, tokens, small, ws, bs, rows):
     items, _, dim = tokens.shape
     width = 2 * ws[0].shape[1]
-    wide_out = jax.ShapeDtypeStruct((items, rows, width), bf)
-    outs = [wide_out] * 4 + [jax.ShapeDtypeStruct((items, 8, rows), f32)]
+    outs = [later((items, rows, width), bf)] * 3 + [
+        jax.ShapeDtypeStruct((items, rows, width), bf),
+        later((items, 8, rows), f32),
+    ]
     specs = [per_item((rows, width))] * 4 + [per_item((8, rows))]
     if first:
-        outs.append(jax.ShapeDtypeStruct((items, rows, dim), bf))
+        outs.append(later((items, rows, dim), bf))
         specs.append(per_item((rows, dim)))
     return pl.pallas_call(
         functools.partial(attend_kernel, first),
@@ -194,7 +196,7 @@
         + [full(small.shape)],
         out_specs=[per_item((rows, dim))] * 3,
         out_shape=[
-            jax.ShapeDtypeStruct((items, rows, dim), f32),
+            later((items, rows, dim), f32),
             jax.ShapeDtypeStruct((items, rows, dim), bf),
             jax.ShapeDtypeStruct((items, rows, dim), bf),
         ],
@@ -677,7 +679,7 @@
     q_b, k_b, v_b, mixed_b, log_b = attend(
         False, counts, tokens3, vectors, w_b, [b_peer, mate(b_peer)], rows
     )
-    mixed_b, out_peer, up_first, bias_peer, down_later = tie(mixed_b, out_peer, up_first, bias_peer, w_down)
+    mixed_b, out_peer, bias_peer, down_later = tie(mixed_b, out_peer, bias_peer, w_down)
     bias_far = mate(bias_peer)
     down_peer = peer(down_later)
     out_a = jnp.concatenate([w_out, out_mate], axis=0)

time: 275 us -> 269 us (0.978)
  waiting for transfers between devices: 75.9 us -> 69.7 us
  local copies, waits for them, and re-layouts: 24.6 us -> 18.6 us
  Pallas kernels: 104 us -> 108 us
    unnamed x123 -> x107, local copies, waits for them, and re-layouts: 19.3 us -> 12.8 us
    ppermute x62, waiting for transfers between devices: 75.9 us -> 69.7 us  [exchange(): return lax.ppermute(x, axis, [(i, i ^ mask) for i in range(size)])]
  transfers between devices with their start and end apart: 62 -> 62, of which waited for: 25 -> 25; matrix products, arithmetic and copies ran while one was open for 6% -> 6% of each run, Pallas kernels for 38% -> 40%
where the time goes in v2:
time: 269 us; the launch traced here: 268 us
  Pallas kernels  108 us (40%)
  waiting for transfers between devices  69.7 us (26%)
  starting transfers between devices  59.3 us (22%)
  local copies, waits for them, and re-layouts  18.6 us (7%)
  other arithmetic  10.8 us (4%)
    ppermute x62, waiting for transfers between devices, exchange(): return lax.ppermute(x, axis, [(i, i ^ mask) for i in range(size)])  69.7 us
    ppermute x62, starting transfers between devices, exchange(): return lax.ppermute(x, axis, [(i, i ^ mask) for i in range(size)])  59.3 us
    pallas_call x2, Pallas kernels, feed(): pl.pallas_call(functools.partial(feed_kernel, again, per), grid_spec=pltp...  35.7 us
    pallas_call x2, Pallas kernels, unattend(): pl.pallas_call(unattend_kernel, grid_spec=pltpu.PrefetchScalarGridSpec(nu...  24.9 us
    pallas_call x2, Pallas kernels, attend(): pl.pallas_call(functools.partial(attend_kernel, first), grid_spec=pltpu.P...  23.4 us
    unnamed x107, local copies, waits for them, and re-layouts  12.8 us
    pallas_call x1, Pallas kernels, unnorm(): pl.pallas_call(unnorm_kernel, grid=(items,), in_specs=[per_item((rows, wi...  7.72 us
    pallas_call x1, Pallas kernels, project(): pl.pallas_call(project_kernel, grid=(items,), in_specs=[per_item((rows, d...  7.21 us
  transfers between devices with their start and end apart: 62, of which 25 were waited for; matrix products, arithmetic and copies ran while one was open for 6% of the time, Pallas kernels for 40%

profile of v2, /device:TPU:8, one launch (start us, length us, event | category | flops | bytes accessed | tf_op | source)
XLA Modules:
  0.0 268.4 jit_solution(17509567532712138666)
XLA Ops:
  11.4 11.2 %attend.2 = (bf16[3,288,384]{2,1,0:T(8,128)(2,1)}, bf16[3,288,384]{2,1,0:T(8,128)(2,1)}, bf16[3,288,384]{2,1,0:T(8,128)(2,1)}, bf16[3,288,384]{2,1,0:T(8,128)(2,...) custom-call(s32[3]{0:T(128)S(1)} %dynamic_slice.78.counts, bf16[3,280,768]{2,1,0:T(8,128)(2,1)S(1)} %bitcast.25, ...), custom_call_target="tpu_custom_call" | custom-call | flops 34500001792 | tf_op jit(solution)/shard_map/attend/pallas_call | solution.py:152
  28.9 12.2 %attend.3 = (bf16[3,288,384]{2,1,0:T(8,128)(2,1)}, bf16[3,288,384]{2,1,0:T(8,128)(2,1)}, bf16[3,288,384]{2,1,0:T(8,128)(2,1)}, bf16[3,288,384]{2,1,0:T(8,128)(2,1)S(1)}, f32[3,8,288]{2,1,0:T(8,128)}) custom-call(s32[3]{0:T(128)S(1)} %dynamic_slice.78.counts, bf16[3,280,768]{2,1,0:T(8,128)(2,1)S(1)} %bitcast.26, f32[6,768]{1,0:T(8,128)S(1)} %reshape.66.small.vectors, ...), custom_call_target="tpu_custom_call" | custom-call | flops 34500001792 | tf_op jit(solution)/shard_map/attend/pallas_call | solution.py:152
  43.4 3.5 %branch.1 = (f32[3,288,768]{2,1,0:T(8,128)}, bf16[3,288,768]{2,1,0:T(8,128)(2,1)S(1)}, bf16[3,288,768]{2,1,0:T(8,128)(2,1)S(1)}) custom-call(bf16[3,280,768]{2,1,0:T(8,128)(2,1)S(1)} %bitcast.27, bf16[3,280,768]{2,1,0:T(8,128)(2,1)S(1)} %bitcast.24, bf16[3,288,384]{2,1,0:T(8,128)(2,1)S(1)} %get-tuple-element.139.mixed_a, ...), custom_call_target="tpu_custom_call" | custom-call | flops 11500000 | tf_op jit(solution)/shard_map/branch/pallas_call | solution.py:190
  48.5 16.3 %feed.2 = (f32[3,288,768]{2,1,0:T(8,128)S(1)}, bf16[3,288,1536]{2,1,0:T(8,128)(2,1)}, bf16[768,768]{1,0:T(8,128)(2,1)S(1)}, bf16[768,768]{1,0:T(8,128)(2,1)S(1)}...) custom-call(s32[1]{0:T(128)} %bitcast.3.low_half, ...), custom_call_target="tpu_custom_call" | custom-call | flops 62100000768 | tf_op jit(solution)/shard_map/feed/pallas_call | solution.py:287
  68.5 3.4 %collective-permute-done.16.refs_4_.refs_2_ = bf16[768,768]{1,0:T(8,128)(2,1)} collective-permute-done((bf16[768,768]{1,0:T(8,128)(2,1)S(1)}, bf16[768,768]{1,0:T(8,128)(2,1)}, u32[]{:S(2)}, u32[]{:S(2)}) %collective-permute-start.16) | collective-permute-done | bytes 1179680 | tf_op jit(solution)/shard_map/ppermute | solution.py:554
  75.9 19.4 %feed.3 = (f32[3,288,768]{2,1,0:T(8,128)S(1)}, bf16[3,288,1536]{2,1,0:T(8,128)(2,1)}, bf16[768,768]{1,0:T(8,128)(2,1)S(1)}, bf16[768,768]{1,0:T(8,128)(2,1)S(1)}...) custom-call(s32[1]{0:T(128)} %bitcast.3.low_half, ...), custom_call_target="tpu_custom_call" | custom-call | flops 62100000768 | tf_op jit(solution)/shard_map/feed/pallas_call | solution.py:287
  95.9 5.9 %unbranch.1 = (f32[3,288,768]{2,1,0:T(8,128)S(1)}, bf16[3,288,384]{2,1,0:T(8,128)(2,1)S(1)}, bf16[3,288,384]{2,1,0:T(8,128)(2,1)S(1)}, bf16[4,192,768]{2,1,0:T(8,128)(2,1)S(1)}, f32[8,768]{1,0:T(8,128)S(1)}) custom-call(f32[3,288,768]{2,1,0:T(8,128)S(1)} %copy-done.11, bf16[3,288,768]{2,1,0:T(8,128)(2,1)S(1)} %copy-done.13, ...), custom_call_target="tpu_custom_call" | custom-call | flops 20700000256 | tf_op jit(solution)/shard_map/unbranch/pallas_call | solution.py:388
  105.3 12.4 %unattend.2 = (bf16[3,288,1152]{2,1,0:T(8,128)(2,1)S(1)}, bf16[2,3,192,768]{3,2,1,0:T(8,128)(2,1)S(1)}, f32[8,384]{1,0:T(8,128)S(1)}) custom-call(s32[3]{0:T(128)S(1)} %copy-done.30, bf16[3,288,384]{2,1,0:T(8,128)(2,1)S(1)} %copy-done.38, bf16[3,288,384]{2,1,0:T(8,128)(2,1)S(1)} %copy-done.39, bf16[3,288,384]{2,1,0:T(8,128)(2,1)S(1)} %copy-done.40, ...), custom_call_target="tpu_custom_call" | custom-call | flops 37950001152 | tf_op jit(solution)/shard_map/unattend/pallas_call | solution.py:469
  126.0 7.2 %project.1 = f32[3,280,768]{2,1,0:T(8,128)} custom-call(f32[3,288,768]{2,1,0:T(8,128)S(1)} %copy-done.11, f32[6,768]{1,0:T(8,128)S(1)} %copy-done.10, bf16[3,288,1536]{2,1,0:T(8,128)(2,1)S(1)} %copy-done.31, bf16[3,288,1536]{2,1,0:T(8,128)(2,1)S(1)} %copy-done.32, bf16[768,768]{1,0:T(8,128)(2,1)S(1)} %copy-done.16, bf16[768,768]{1,0:T(8,128)(2,1)S(1)} %copy-done.18, ...), custom_call_target="tpu_custom_call" | custom-call | flops 20700000256 | tf_op jit(solution)/shard_map/project/pallas_call | solution.py:336
  139.8 2.6 collective-permute-start.35
  144.9 12.4 %unattend.3 = (bf16[3,288,1152]{2,1,0:T(8,128)(2,1)S(1)}, bf16[2,3,192,768]{3,2,1,0:T(8,128)(2,1)S(1)}, f32[8,384]{1,0:T(8,128)S(1)}) custom-call(s32[3]{0:T(128)S(1)} %copy-done.30, bf16[3,288,384]{2,1,0:T(8,128)(2,1)S(1)} %copy-done.35, bf16[3,288,384]{2,1,0:T(8,128)(2,1)S(1)} %copy-done.36, bf16[3,288,384]{2,1,0:T(8,128)(2,1)S(1)} %copy-done.37, ...), custom_call_target="tpu_custom_call" | custom-call | flops 37950001152 | tf_op jit(solution)/shard_map/unattend/pallas_call | solution.py:469
  158.5 2.6 collective-permute-start.41
  167.5 7.7 %unnorm.1 = (f32[3,280,768]{2,1,0:T(8,128)}, f32[8,768]{1,0:T(8,128)S(1)}) custom-call(bf16[3,288,1152]{2,1,0:T(8,128)(2,1)S(1)} %get-tuple-element.238.g_a, bf16[3,288,1152]{2,1,0:T(8,128)(2,1)S(1)} %get-tuple-element.239.g_b, bf16[3,192,768]{2,1,0:T(8,128)(2,1)S(1)} %bitcast.32, bf16[3,192,768]{2,1,0:T(8,128)(2,1)S(1)} %copy-done.24, ...), custom_call_target="tpu_custom_call" | custom-call | flops 20700000256 | tf_op jit(solution)/shard_map/unnorm/pallas_call | solution.py:512
  176.9 9.2 %collective-permute-done.38 = bf16[320,768]{1,0:T(8,128)(2,1)S(1)} collective-permute-done((bf16[320,768]{1,0:T(8,128)(2,1)S(1)}, bf16[320,768]{1,0:T(8,128)(2,1)S(1)}, u32[]{:S(2)}, u32[]{:S(2)}) %collective-permute-start.38) | collective-permute-done | bytes 491552 | tf_op jit(solution)/shard_map/ppermute | solution.py:554
  187.5 4.4 %collective-permute-start.55 = (bf16[120,768]{1,0:T(8,128)(2,1)S(1)}, bf16[120,768]{1,0:T(8,128)(2,1)S(1)}, u32[]{:S(2)}, u32[]{:S(2)}) collective-permute-start(bf16[120,768]{1,0:T(8,128)(2,1)S(1)} %get-tuple-element.305), channel_id=1, source_target_pairs={{0,16},{4,20},{8,24},{12,28},{16,0},{20,4},{24,8},{28,12},{1,17},{... | collective-permute-start | bytes 552968 | tf_op jit(solution)/shard_map/ppermute | solution.py:554
  197.2 2.1 collective-permute-done.46
  200.6 2.6 collective-permute-start.47
  203.2 11.0 %collective-permute-done.49 = bf16[80,768]{1,0:T(8,128)(2,1)S(1)} collective-permute-done((bf16[80,768]{1,0:T(8,128)(2,1)S(1)}, bf16[80,768]{1,0:T(8,128)(2,1)S(1)}, u32[]{:S(2)}, u32[]{:S(2)}) %collective-permute-start.49) | collective-permute-done | bytes 122912 | tf_op jit(solution)/shard_map/ppermute | solution.py:554
  216.1 3.6 %collective-permute-start.50 = (bf16[80,768]{1,0:T(8,128)(2,1)S(1)}, bf16[80,768]{1,0:T(8,128)(2,1)S(1)}, u32[]{:S(2)}, u32[]{:S(2)}) collective-permute-start(bf16[80,768]{1,0:T(8,128)(2,1)S(1)} %get-tuple-element.275), channel_id=1, source_target_pairs={{0,8},{4,12},{8,0},{12,4},{16,24},{20,28},{24,16},{28,20},{1,9},{5... | collective-permute-start | bytes 368648 | tf_op jit(solution)/shard_map/ppermute | solution.py:554
  221.5 2.9 %collective-permute-start.57 = (bf16[120,768]{1,0:T(8,128)(2,1)S(1)}, bf16[120,768]{1,0:T(8,128)(2,1)S(1)}, u32[]{:S(2)}, u32[]{:S(2)}) collective-permute-start(bf16[120,768]{1,0:T(8,128)(2,1)S(1)} %get-tuple-element.273), channel_id=1, source_target_pairs={{0,8},{4,12},{8,0},{12,4},{16,24},{20,28},{24,16},{28,20},{1,9},{5... | collective-permute-start | bytes 552968 | tf_op jit(solution)/shard_map/ppermute | solution.py:554
  224.4 2.6 collective-permute-start.58
  230.1 10.9 %collective-permute-done.52 = bf16[80,768]{1,0:T(8,128)(2,1)S(1)} collective-permute-done((bf16[80,768]{1,0:T(8,128)(2,1)S(1)}, bf16[80,768]{1,0:T(8,128)(2,1)S(1)}, u32[]{:S(2)}, u32[]{:S(2)}) %collective-permute-start.52) | collective-permute-done | bytes 122912 | tf_op jit(solution)/shard_map/ppermute | solution.py:554
  243.1 4.4 %collective-permute-done.59 = bf16[120,768]{1,0:T(8,128)(2,1)S(1)} collective-permute-done((bf16[120,768]{1,0:T(8,128)(2,1)S(1)}, bf16[120,768]{1,0:T(8,128)(2,1)S(1)}, u32[]{:S(2)}, u32[]{:S(2)}) %collective-permute-start.59) | collective-permute-done | bytes 184352 | tf_op jit(solution)/shard_map/ppermute | solution.py:554
  254.8 11.0 %collective-permute-done.60 = bf16[480,768]{1,0:T(8,128)(2,1)S(1)} collective-permute-done((bf16[480,768]{1,0:T(8,128)(2,1)S(1)}, bf16[480,768]{1,0:T(8,128)(2,1)S(1)}, u32[]{:S(2)}, u32[]{:S(2)}) %collective-permute-start.60) | collective-permute-done | bytes 737312 | tf_op jit(solution)/shard_map/ppermute | solution.py:554
  (303 shorter events, 85.3 us)
Async XLA Ops:
  0.7 22.4 %collective-permute-start.2 = (bf16[3,192,768]{2,1,0:T(8,128)(2,1)}, bf16[3,192,768]{2,1,0:T(8,128)(2,1)}, u32[]{:S(2)}, u32[]{:S(2)}) collective-permute-start(bf16[3,192,768]{2,1,0:T(8,128)(2,1)} %bitcast.30), channel_id=1, source_target_pairs={{0,2},{1,3},{2,0},{3,1},{4,6},{5,7},{6,4},{7,5},{8,10},{9,11},{10,... | collective-permute-start | bytes 2654216 | tf_op jit(solution)/shard_map/ppermute | solution.py:554
  2.5 20.7 %collective-permute-start.3 = (f32[2,192]{1,0:T(2,128)}, f32[2,192]{1,0:T(2,128)S(1)}, u32[]{:S(2)}, u32[]{:S(2)}) collective-permute-start(f32[2,192]{1,0:T(2,128)} %b_one.1), channel_id=1, source_target_pairs={{0,2},{1,3},{2,0},{3,1},{4,6},{5,7},{6,4},{7,5},{8,10},{9,11},{10,... | collective-permute-start | bytes 4616 | tf_op jit(solution)/shard_map/ppermute | solution.py:554
  25.7 22.8 %collective-permute-start.11 = (bf16[768,768]{1,0:T(8,128)(2,1)S(1)}, bf16[768,768]{1,0:T(8,128)(2,1)S(1)}, u32[]{:S(2)}, u32[]{:S(2)}) collective-permute-start(bf16[768,768]{1,0:T(8,128)(2,1)S(1)} %copy-done.8), channel_id=1, source_target_pairs={{0,1},{1,0},{2,3},{3,2},{4,5},{5,4},{6,7},{7,6},{8,9},{9,8},{10,11... | collective-permute-start | bytes 3538952 | tf_op jit(solution)/shard_map/ppermute | solution.py:554
  27.2 19.8 %collective-permute-start.10 = (bf16[384,768]{1,0:T(8,128)(2,1)S(1)}, bf16[384,768]{1,0:T(8,128)(2,1)S(1)}, u32[]{:S(2)}, u32[]{:S(2)}) collective-permute-start(bf16[384,768]{1,0:T(8,128)(2,1)S(1)} %constant_dynamic-slice_fusion.19), channel_id=1, source_target_pairs={{0,2},{1,3},{2,0},{3,1},{4,6},{5,7},{6,4},{7,5},{8,10},{9,11},{10,... | collective-permute-start | bytes 1769480 | tf_op jit(solution)/shard_map/ppermute | solution.py:554
  28.8 19.7 %collective-permute-start.12 = (bf16[768,768]{1,0:T(8,128)(2,1)S(1)}, bf16[768,768]{1,0:T(8,128)(2,1)S(1)}, u32[]{:S(2)}, u32[]{:S(2)}) collective-permute-start(bf16[768,768]{1,0:T(8,128)(2,1)S(1)} %copy-done.15), channel_id=1, source_target_pairs={{0,1},{1,0},{2,3},{3,2},{4,5},{5,4},{6,7},{7,6},{8,9},{9,8},{10,11... | collective-permute-start | bytes 3538952 | tf_op jit(solution)/shard_map/ppermute | solution.py:554
  42.9 29.0 %collective-permute-start.16 = (bf16[768,768]{1,0:T(8,128)(2,1)S(1)}, bf16[768,768]{1,0:T(8,128)(2,1)}, u32[]{:S(2)}, u32[]{:S(2)}) collective-permute-start(bf16[768,768]{1,0:T(8,128)(2,1)S(1)} %copy-done.15), channel_id=1, source_target_pairs={{0,2},{1,3},{2,0},{3,1},{4,6},{5,7},{6,4},{7,5},{8,10},{9,11},{10,... | collective-permute-start | bytes 3538952 | tf_op jit(solution)/shard_map/ppermute | solution.py:554
  47.0 21.5 %collective-permute-start.14 = (bf16[384,768]{1,0:T(8,128)(2,1)S(1)}, bf16[384,768]{1,0:T(8,128)(2,1)}, u32[]{:S(2)}, u32[]{:S(2)}) collective-permute-start(bf16[384,768]{1,0:T(8,128)(2,1)S(1)} %collective-permute-done.10.refs_0_), channel_id=1, source_target_pairs={{0,4},{4,0},{8,12},{12,8},{16,20},{20,16},{24,28},{28,24},{1,5},{5... | collective-permute-start | bytes 1769480 | tf_op jit(solution)/shard_map/ppermute | solution.py:554
  48.5 20.0 %collective-permute-start.15 = (bf16[384,768]{1,0:T(8,128)(2,1)S(1)}, bf16[384,768]{1,0:T(8,128)(2,1)S(1)}, u32[]{:S(2)}, u32[]{:S(2)}) collective-permute-start(bf16[384,768]{1,0:T(8,128)(2,1)S(1)} %collective-permute-done.10.refs_0_), channel_id=1, source_target_pairs={{0,1},{1,0},{2,3},{3,2},{4,5},{5,4},{6,7},{7,6},{8,9},{9,8},{10,11... | collective-permute-start | bytes 1769480 | tf_op jit(solution)/shard_map/ppermute | solution.py:554
  73.5 21.8 %collective-permute-start.20 = (bf16[768,768]{1,0:T(8,128)(2,1)}, bf16[768,768]{1,0:T(8,128)(2,1)S(1)}, u32[]{:S(2)}, u32[]{:S(2)}) collective-permute-start(bf16[768,768]{1,0:T(8,128)(2,1)} %copy-done.20), channel_id=1, source_target_pairs={{0,1},{1,0},{2,3},{3,2},{4,5},{5,4},{6,7},{7,6},{8,9},{9,8},{10,11... | collective-permute-start | bytes 3538952 | tf_op jit(solution)/shard_map/ppermute | solution.py:554
  74.1 21.2 %collective-permute-start.21 = (bf16[768,768]{1,0:T(8,128)(2,1)}, bf16[768,768]{1,0:T(8,128)(2,1)S(1)}, u32[]{:S(2)}, u32[]{:S(2)}) collective-permute-start(bf16[768,768]{1,0:T(8,128)(2,1)} %copy-done.19), channel_id=1, source_target_pairs={{0,1},{1,0},{2,3},{3,2},{4,5},{5,4},{6,7},{7,6},{8,9},{9,8},{10,11... | collective-permute-start | bytes 3538952 | tf_op jit(solution)/shard_map/ppermute | solution.py:554
  118.6 18.4 %collective-permute-start.28 = (bf16[640,768]{1,0:T(8,128)(2,1)S(1)}, bf16[640,768]{1,0:T(8,128)(2,1)S(1)}, u32[]{:S(2)}, u32[]{:S(2)}) collective-permute-start(bf16[640,768]{1,0:T(8,128)(2,1)S(1)} %fusion.5), channel_id=1, source_target_pairs={{0,1},{1,0},{2,3},{3,2},{4,5},{5,4},{6,7},{7,6},{8,9},{9,8},{10,11... | collective-permute-start | bytes 2949128 | tf_op jit(solution)/shard_map/ppermute | solution.py:554
  122.8 20.5 %collective-permute-start.32 = (bf16[192,768]{1,0:T(8,128)(2,1)S(1)}, bf16[192,768]{1,0:T(8,128)(2,1)S(1)}, u32[]{:S(2)}, u32[]{:S(2)}) collective-permute-start(bf16[192,768]{1,0:T(8,128)(2,1)S(1)} %get-tuple-element.311), channel_id=1, source_target_pairs={{0,4},{4,0},{8,12},{12,8},{16,20},{20,16},{24,28},{28,24},{1,5},{5... | collective-permute-start | bytes 884744 | tf_op jit(solution)/shard_map/ppermute | solution.py:554
  123.9 33.5 %collective-permute-start.33 = (bf16[576,768]{1,0:T(8,128)(2,1)S(1)}, bf16[576,768]{1,0:T(8,128)(2,1)S(1)}, u32[]{:S(2)}, u32[]{:S(2)}) collective-permute-start(bf16[576,768]{1,0:T(8,128)(2,1)S(1)} %pad_maximum_fusion.4), channel_id=1, source_target_pairs={{0,2},{1,3},{2,0},{3,1},{4,6},{5,7},{6,4},{7,5},{8,10},{9,11},{10,... | collective-permute-start | bytes 2654216 | tf_op jit(solution)/shard_map/ppermute | solution.py:554
  137.4 20.0 %collective-permute-start.31 = (bf16[320,768]{1,0:T(8,128)(2,1)S(1)}, bf16[320,768]{1,0:T(8,128)(2,1)S(1)}, u32[]{:S(2)}, u32[]{:S(2)}) collective-permute-start(bf16[320,768]{1,0:T(8,128)(2,1)S(1)} %get-tuple-element.298), channel_id=1, source_target_pairs={{0,4},{4,0},{8,12},{12,8},{16,20},{20,16},{24,28},{28,24},{1,5},{5... | collective-permute-start | bytes 1474568 | tf_op jit(solution)/shard_map/ppermute | solution.py:554
  139.3 18.1 %collective-permute-start.34 = (bf16[96,768]{1,0:T(8,128)(2,1)S(1)}, bf16[96,768]{1,0:T(8,128)(2,1)S(1)}, u32[]{:S(2)}, u32[]{:S(2)}) collective-permute-start(bf16[96,768]{1,0:T(8,128)(2,1)S(1)} %get-tuple-element.309), channel_id=1, source_target_pairs={{0,8},{4,12},{8,0},{12,4},{16,24},{20,28},{24,16},{28,20},{1,9},{5... | collective-permute-start | bytes 442376 | tf_op jit(solution)/shard_map/ppermute | solution.py:554
  166.0 20.1 %collective-permute-start.38 = (bf16[320,768]{1,0:T(8,128)(2,1)S(1)}, bf16[320,768]{1,0:T(8,128)(2,1)S(1)}, u32[]{:S(2)}, u32[]{:S(2)}) collective-permute-start(bf16[320,768]{1,0:T(8,128)(2,1)S(1)} %get-tuple-element.296), channel_id=1, source_target_pairs={{0,4},{4,0},{8,12},{12,8},{16,20},{20,16},{24,28},{28,24},{1,5},{5... | collective-permute-start | bytes 1474568 | tf_op jit(solution)/shard_map/ppermute | solution.py:554
  186.9 32.7 %collective-permute-start.56 = (bf16[120,768]{1,0:T(8,128)(2,1)S(1)}, bf16[120,768]{1,0:T(8,128)(2,1)S(1)}, u32[]{:S(2)}, u32[]{:S(2)}) collective-permute-start(bf16[120,768]{1,0:T(8,128)(2,1)S(1)} %get-tuple-element.306), channel_id=1, source_target_pairs={{0,24},{4,28},{8,16},{12,20},{16,8},{20,12},{24,0},{28,4},{1,25},{... | collective-permute-start | bytes 552968 | tf_op jit(solution)/shard_map/ppermute | solution.py:554
  187.5 32.2 %collective-permute-start.55 = (bf16[120,768]{1,0:T(8,128)(2,1)S(1)}, bf16[120,768]{1,0:T(8,128)(2,1)S(1)}, u32[]{:S(2)}, u32[]{:S(2)}) collective-permute-start(bf16[120,768]{1,0:T(8,128)(2,1)S(1)} %get-tuple-element.305), channel_id=1, source_target_pairs={{0,16},{4,20},{8,24},{12,28},{16,0},{20,4},{24,8},{28,12},{1,17},{... | collective-permute-start | bytes 552968 | tf_op jit(solution)/shard_map/ppermute | solution.py:554
  214.4 33.7 %collective-permute-start.61 = (bf16[384,768]{1,0:T(8,128)(2,1)S(1)}, bf16[384,768]{1,0:T(8,128)(2,1)S(1)}, u32[]{:S(2)}, u32[]{:S(2)}) collective-permute-start(bf16[384,768]{1,0:T(8,128)(2,1)S(1)} %constant_dynamic-update-slice_fusion.5), channel_id=1, source_target_pairs={{0,4},{4,0},{8,12},{12,8},{16,20},{20,16},{24,28},{28,24},{1,5},{5... | collective-permute-start | bytes 1769480 | tf_op jit(solution)/shard_map/ppermute | solution.py:554
  219.7 21.3 %collective-permute-start.52 = (bf16[80,768]{1,0:T(8,128)(2,1)S(1)}, bf16[80,768]{1,0:T(8,128)(2,1)S(1)}, u32[]{:S(2)}, u32[]{:S(2)}) collective-permute-start(bf16[80,768]{1,0:T(8,128)(2,1)S(1)} %get-tuple-element.275), channel_id=1, source_target_pairs={{0,24},{4,28},{8,16},{12,20},{16,8},{20,12},{24,0},{28,4},{1,25},{... | collective-permute-start | bytes 368648 | tf_op jit(solution)/shard_map/ppermute | solution.py:554
  221.5 20.2 %collective-permute-start.57 = (bf16[120,768]{1,0:T(8,128)(2,1)S(1)}, bf16[120,768]{1,0:T(8,128)(2,1)S(1)}, u32[]{:S(2)}, u32[]{:S(2)}) collective-permute-start(bf16[120,768]{1,0:T(8,128)(2,1)S(1)} %get-tuple-element.273), channel_id=1, source_target_pairs={{0,8},{4,12},{8,0},{12,4},{16,24},{20,28},{24,16},{28,20},{1,9},{5... | collective-permute-start | bytes 552968 | tf_op jit(solution)/shard_map/ppermute | solution.py:554
  224.4 18.6 %collective-permute-start.58 = (bf16[120,768]{1,0:T(8,128)(2,1)S(1)}, bf16[120,768]{1,0:T(8,128)(2,1)S(1)}, u32[]{:S(2)}, u32[]{:S(2)}) collective-permute-start(bf16[120,768]{1,0:T(8,128)(2,1)S(1)} %get-tuple-element.273), channel_id=1, source_target_pairs={{0,16},{4,20},{8,24},{12,28},{16,0},{20,4},{24,8},{28,12},{1,17},{... | collective-permute-start | bytes 552968 | tf_op jit(solution)/shard_map/ppermute | solution.py:554
  228.4 19.1 %collective-permute-start.59 = (bf16[120,768]{1,0:T(8,128)(2,1)S(1)}, bf16[120,768]{1,0:T(8,128)(2,1)S(1)}, u32[]{:S(2)}, u32[]{:S(2)}) collective-permute-start(bf16[120,768]{1,0:T(8,128)(2,1)S(1)} %get-tuple-element.273), channel_id=1, source_target_pairs={{0,24},{4,28},{8,16},{12,20},{16,8},{20,12},{24,0},{28,4},{1,25},{... | collective-permute-start | bytes 552968 | tf_op jit(solution)/shard_map/ppermute | solution.py:554
  247.5 18.2 %collective-permute-start.60 = (bf16[480,768]{1,0:T(8,128)(2,1)S(1)}, bf16[480,768]{1,0:T(8,128)(2,1)S(1)}, u32[]{:S(2)}, u32[]{:S(2)}) collective-permute-start(bf16[480,768]{1,0:T(8,128)(2,1)S(1)} %constant_dynamic-update-slice_fusion.9), channel_id=1, source_target_pairs={{0,4},{4,0},{8,12},{12,8},{16,20},{20,16},{24,28},{28,24},{1,5},{5... | collective-permute-start | bytes 2211848 | tf_op jit(solution)/shard_map/ppermute | solution.py:554
  (88 other events, 837.5 us)

commit v3 on v2

--- a/solution.py
+++ b/solution.py
@@ -412,7 +412,7 @@
     )(middle, cot, grad_in, vectors, mixed_a, mixed_b, w_a, w_b)
 
 
-def unattend_kernel(counts, q, k, v, gmix, logs, normed, g_ref, dw_out, db_out):
+def unattend_kernel(unroll, counts, q, k, v, gmix, logs, normed, g_ref, dw_out, db_out):
     step = pl.program_id(0)
     rows, width = q.shape
     valid = WORDS + counts[step]
@@ -439,7 +439,7 @@
             g_ref[step, :, pl.ds(pl.multiple_of(c * width + p * LANES, LANES), LANES)] = merged
         return carry
 
-    lax.fori_loop(0, width // LANES, one_pair, 0)
+    lax.fori_loop(0, width // LANES, one_pair, 0, unroll=unroll)
 
     @pl.when(step == 0)
     def _():
@@ -463,11 +463,11 @@
         lax.fori_loop(0, 3, one_kind, 0)
 
 
-def unattend(counts, q, k, v, gmix, logs, normed):
+def unattend(unroll, counts, q, k, v, gmix, logs, normed):
     items, rows, width = q.shape
     dim = normed.shape[2]
     return pl.pallas_call(
-        unattend_kernel,
+        functools.partial(unattend_kernel, unroll),
         grid_spec=pltpu.PrefetchScalarGridSpec(
             num_scalar_prefetch=1,
             grid=(items,),
@@ -721,7 +721,7 @@
     up_one = peer(add_bf(top(dup_peer), top(far_up)))
     pair_keep, pair_got = ring.send(x_axis, add_bf(ddown_peer, far_down))
     out_far, out_near = mate(dw_out[3]), mate(dw_out[1])
-    g_b, dqkv_b, dbqv_b = unattend(counts, q_b, k_b, v_b, gmix_b, log_b, normed1)
+    g_b, dqkv_b, dbqv_b = unattend(False, counts, q_b, k_b, v_b, gmix_b, log_b, normed1)
     g_b, dqkv_b, dbqv_b, up_one, pair_keep, pair_got, ddown_own, got_down, out_far, out_near, far_up, dup_peer = tie(
         g_b, dqkv_b, dbqv_b, up_one, pair_keep, pair_got, ddown_own, got_down, out_far, out_near, far_up, dup_peer
     )
@@ -752,7 +752,7 @@
     )
     rest_keep, rest_got = ring.send(x_axis, add_bf(block(2, dqkv_b, dbqv_b, dbias_b), far_rest))
     down_parts = ring.send(z_axis, add_bf(down_keep, down_got, pair_half))
-    g_a, dqkv_a, dbqv_a = unattend(counts, q_a, k_a, v_a, gmix_a, log_a, normed1)
+    g_a, dqkv_a, dbqv_a = unattend(True, counts, q_a, k_a, v_a, gmix_a, log_a, normed1)
     g_a, dqkv_a, dbqv_a, rest_keep, rest_got, one_keep, one_got, two_got, *down_parts = tie(
         g_a, dqkv_a, dbqv_a, rest_keep, rest_got, one_keep, one_got, two_got, *down_parts
     )
@@ -770,11 +770,12 @@
         small_one, rest_keep, rest_got, rest_half, two_keep, two_got, *down_all
     )
     down_sum = ring.place(z_axis, down_all)
+    up_half = jnp.concatenate([add_bf(one_keep, one_got), add_bf(two_keep, two_got)], axis=0)
+    small_one, up_half = tie(small_one, up_half)
     firsts = small_one[0:2]
     firsts = firsts + mate(firsts)
     firsts = firsts + peer(firsts)
     firsts = firsts + across(firsts)
-    up_half = jnp.concatenate([add_bf(one_keep, one_got), add_bf(two_keep, two_got)], axis=0)
     rest_sum = add_bf(rest_keep, rest_got, rest_half)
     spot = lax.broadcasted_iota(jnp.int32, (rest_sum.shape[0], 1), 0) - (
         3 * heads + 7 - low_half * rest_sum.shape[0]

time: 269 us -> 267 us (level)
  no operation moved by 1% of the time
where the time goes in v3:
time: 267 us
  Pallas kernels  107 us (40%)
  waiting for transfers between devices  69.6 us (26%)
  starting transfers between devices  59.5 us (22%)
  local copies, waits for them, and re-layouts  18.7 us (7%)
  other arithmetic  10.1 us (4%)
    ppermute x62, waiting for transfers between devices, exchange(): return lax.ppermute(x, axis, [(i, i ^ mask) for i in range(size)])  69.6 us
    ppermute x62, starting transfers between devices, exchange(): return lax.ppermute(x, axis, [(i, i ^ mask) for i in range(size)])  59.5 us
    pallas_call x2, Pallas kernels, feed(): pl.pallas_call(functools.partial(feed_kernel, again, per), grid_spec=pltp...  35.7 us
    pallas_call x2, Pallas kernels, unattend(): pl.pallas_call(functools.partial(unattend_kernel, unroll), grid_spec=pltp...  23.9 us
    pallas_call x2, Pallas kernels, attend(): pl.pallas_call(functools.partial(attend_kernel, first), grid_spec=pltpu.P...  23.4 us
    unnamed x107, local copies, waits for them, and re-layouts  12.8 us
    pallas_call x1, Pallas kernels, unnorm(): pl.pallas_call(unnorm_kernel, grid=(items,), in_specs=[per_item((rows, wi...  7.72 us
    pallas_call x1, Pallas kernels, project(): pl.pallas_call(project_kernel, grid=(items,), in_specs=[per_item((rows, d...  7.21 us
  transfers between devices with their start and end apart: 62, of which 25 were waited for; matrix products, arithmetic and copies ran while one was open for 6% of the time, Pallas kernels for 40%

profile of v3, /device:TPU:8, one launch (start us, length us, event | category | flops | bytes accessed | tf_op | source)
XLA Modules:
  0.0 266.8 jit_solution(6961350718678053666)
XLA Ops:
  11.4 11.2 %attend.2 = (bf16[3,288,384]{2,1,0:T(8,128)(2,1)}, bf16[3,288,384]{2,1,0:T(8,128)(2,1)}, bf16[3,288,384]{2,1,0:T(8,128)(2,1)}, bf16[3,288,384]{2,1,0:T(8,128)(2,...) custom-call(s32[3]{0:T(128)S(1)} %dynamic_slice.78.counts, bf16[3,280,768]{2,1,0:T(8,128)(2,1)S(1)} %bitcast.25, ...), custom_call_target="tpu_custom_call" | custom-call | flops 34500001792 | tf_op jit(solution)/shard_map/attend/pallas_call | solution.py:152
  28.9 12.2 %attend.3 = (bf16[3,288,384]{2,1,0:T(8,128)(2,1)}, bf16[3,288,384]{2,1,0:T(8,128)(2,1)}, bf16[3,288,384]{2,1,0:T(8,128)(2,1)}, bf16[3,288,384]{2,1,0:T(8,128)(2,1)S(1)}, f32[3,8,288]{2,1,0:T(8,128)}) custom-call(s32[3]{0:T(128)S(1)} %dynamic_slice.78.counts, bf16[3,280,768]{2,1,0:T(8,128)(2,1)S(1)} %bitcast.26, f32[6,768]{1,0:T(8,128)S(1)} %reshape.66.small.vectors, ...), custom_call_target="tpu_custom_call" | custom-call | flops 34500001792 | tf_op jit(solution)/shard_map/attend/pallas_call | solution.py:152
  43.4 3.5 %branch.1 = (f32[3,288,768]{2,1,0:T(8,128)}, bf16[3,288,768]{2,1,0:T(8,128)(2,1)S(1)}, bf16[3,288,768]{2,1,0:T(8,128)(2,1)S(1)}) custom-call(bf16[3,280,768]{2,1,0:T(8,128)(2,1)S(1)} %bitcast.27, bf16[3,280,768]{2,1,0:T(8,128)(2,1)S(1)} %bitcast.24, bf16[3,288,384]{2,1,0:T(8,128)(2,1)S(1)} %get-tuple-element.141.mixed_a, ...), custom_call_target="tpu_custom_call" | custom-call | flops 11500000 | tf_op jit(solution)/shard_map/branch/pallas_call | solution.py:190
  48.5 16.3 %feed.2 = (f32[3,288,768]{2,1,0:T(8,128)S(1)}, bf16[3,288,1536]{2,1,0:T(8,128)(2,1)}, bf16[768,768]{1,0:T(8,128)(2,1)S(1)}, bf16[768,768]{1,0:T(8,128)(2,1)S(1)}...) custom-call(s32[1]{0:T(128)} %bitcast.3.low_half, ...), custom_call_target="tpu_custom_call" | custom-call | flops 62100000768 | tf_op jit(solution)/shard_map/feed/pallas_call | solution.py:287
  68.5 3.4 %collective-permute-done.16.refs_4_.refs_2_ = bf16[768,768]{1,0:T(8,128)(2,1)} collective-permute-done((bf16[768,768]{1,0:T(8,128)(2,1)S(1)}, bf16[768,768]{1,0:T(8,128)(2,1)}, u32[]{:S(2)}, u32[]{:S(2)}) %collective-permute-start.16) | collective-permute-done | bytes 1179680 | tf_op jit(solution)/shard_map/ppermute | solution.py:554
  75.9 19.4 %feed.3 = (f32[3,288,768]{2,1,0:T(8,128)S(1)}, bf16[3,288,1536]{2,1,0:T(8,128)(2,1)}, bf16[768,768]{1,0:T(8,128)(2,1)S(1)}, bf16[768,768]{1,0:T(8,128)(2,1)S(1)}...) custom-call(s32[1]{0:T(128)} %bitcast.3.low_half, ...), custom_call_target="tpu_custom_call" | custom-call | flops 62100000768 | tf_op jit(solution)/shard_map/feed/pallas_call | solution.py:287
  95.9 5.9 %unbranch.1 = (f32[3,288,768]{2,1,0:T(8,128)S(1)}, bf16[3,288,384]{2,1,0:T(8,128)(2,1)S(1)}, bf16[3,288,384]{2,1,0:T(8,128)(2,1)S(1)}, bf16[4,192,768]{2,1,0:T(8,128)(2,1)S(1)}, f32[8,768]{1,0:T(8,128)S(1)}) custom-call(f32[3,288,768]{2,1,0:T(8,128)S(1)} %copy-done.11, bf16[3,288,768]{2,1,0:T(8,128)(2,1)S(1)} %copy-done.13, ...), custom_call_target="tpu_custom_call" | custom-call | flops 20700000256 | tf_op jit(solution)/shard_map/unbranch/pallas_call | solution.py:388
  105.3 12.4 %unattend.2 = (bf16[3,288,1152]{2,1,0:T(8,128)(2,1)S(1)}, bf16[2,3,192,768]{3,2,1,0:T(8,128)(2,1)S(1)}, f32[8,384]{1,0:T(8,128)S(1)}) custom-call(s32[3]{0:T(128)S(1)} %copy-done.30, bf16[3,288,384]{2,1,0:T(8,128)(2,1)S(1)} %copy-done.38, bf16[3,288,384]{2,1,0:T(8,128)(2,1)S(1)} %copy-done.39, bf16[3,288,384]{2,1,0:T(8,128)(2,1)S(1)} %copy-done.40, ...), custom_call_target="tpu_custom_call" | custom-call | flops 37950001152 | tf_op jit(solution)/shard_map/unattend/pallas_call | solution.py:469
  126.0 7.2 %project.1 = f32[3,280,768]{2,1,0:T(8,128)} custom-call(f32[3,288,768]{2,1,0:T(8,128)S(1)} %copy-done.11, f32[6,768]{1,0:T(8,128)S(1)} %copy-done.10, bf16[3,288,1536]{2,1,0:T(8,128)(2,1)S(1)} %copy-done.31, bf16[3,288,1536]{2,1,0:T(8,128)(2,1)S(1)} %copy-done.32, bf16[768,768]{1,0:T(8,128)(2,1)S(1)} %copy-done.16, bf16[768,768]{1,0:T(8,128)(2,1)S(1)} %copy-done.18, ...), custom_call_target="tpu_custom_call" | custom-call | flops 20700000256 | tf_op jit(solution)/shard_map/project/pallas_call | solution.py:336
  139.8 2.6 collective-permute-start.35
  144.9 11.4 %unattend.3 = (bf16[3,288,1152]{2,1,0:T(8,128)(2,1)S(1)}, bf16[2,3,192,768]{3,2,1,0:T(8,128)(2,1)S(1)}, f32[8,384]{1,0:T(8,128)S(1)}) custom-call(s32[3]{0:T(128)S(1)} %copy-done.30, bf16[3,288,384]{2,1,0:T(8,128)(2,1)S(1)} %copy-done.35, bf16[3,288,384]{2,1,0:T(8,128)(2,1)S(1)} %copy-done.36, bf16[3,288,384]{2,1,0:T(8,128)(2,1)S(1)} %copy-done.37, ...), custom_call_target="tpu_custom_call" | custom-call | flops 37950001152 | tf_op jit(solution)/shard_map/unattend/pallas_call | solution.py:469
  157.5 2.5 collective-permute-start.41
  166.5 7.7 %unnorm.1 = (f32[3,280,768]{2,1,0:T(8,128)}, f32[8,768]{1,0:T(8,128)S(1)}) custom-call(bf16[3,288,1152]{2,1,0:T(8,128)(2,1)S(1)} %get-tuple-element.240.g_a, bf16[3,288,1152]{2,1,0:T(8,128)(2,1)S(1)} %get-tuple-element.241.g_b, bf16[3,192,768]{2,1,0:T(8,128)(2,1)S(1)} %bitcast.32, bf16[3,192,768]{2,1,0:T(8,128)(2,1)S(1)} %copy-done.24, ...), custom_call_target="tpu_custom_call" | custom-call | flops 20700000256 | tf_op jit(solution)/shard_map/unnorm/pallas_call | solution.py:512
  175.9 9.2 %collective-permute-done.38 = bf16[320,768]{1,0:T(8,128)(2,1)S(1)} collective-permute-done((bf16[320,768]{1,0:T(8,128)(2,1)S(1)}, bf16[320,768]{1,0:T(8,128)(2,1)S(1)}, u32[]{:S(2)}, u32[]{:S(2)}) %collective-permute-start.38) | collective-permute-done | bytes 491552 | tf_op jit(solution)/shard_map/ppermute | solution.py:554
  186.0 4.4 %collective-permute-start.55 = (bf16[120,768]{1,0:T(8,128)(2,1)S(1)}, bf16[120,768]{1,0:T(8,128)(2,1)S(1)}, u32[]{:S(2)}, u32[]{:S(2)}) collective-permute-start(bf16[120,768]{1,0:T(8,128)(2,1)S(1)} %get-tuple-element.310), channel_id=1, source_target_pairs={{0,16},{4,20},{8,24},{12,28},{16,0},{20,4},{24,8},{28,12},{1,17},{... | collective-permute-start | bytes 552968 | tf_op jit(solution)/shard_map/ppermute | solution.py:554
  195.6 2.1 collective-permute-done.46
  199.1 2.5 collective-permute-start.47
  201.7 11.0 %collective-permute-done.49 = bf16[80,768]{1,0:T(8,128)(2,1)S(1)} collective-permute-done((bf16[80,768]{1,0:T(8,128)(2,1)S(1)}, bf16[80,768]{1,0:T(8,128)(2,1)S(1)}, u32[]{:S(2)}, u32[]{:S(2)}) %collective-permute-start.49) | collective-permute-done | bytes 122912 | tf_op jit(solution)/shard_map/ppermute | solution.py:554
  214.5 3.6 %collective-permute-start.50 = (bf16[80,768]{1,0:T(8,128)(2,1)S(1)}, bf16[80,768]{1,0:T(8,128)(2,1)S(1)}, u32[]{:S(2)}, u32[]{:S(2)}) collective-permute-start(bf16[80,768]{1,0:T(8,128)(2,1)S(1)} %get-tuple-element.279), channel_id=1, source_target_pairs={{0,8},{4,12},{8,0},{12,4},{16,24},{20,28},{24,16},{28,20},{1,9},{5... | collective-permute-start | bytes 368648 | tf_op jit(solution)/shard_map/ppermute | solution.py:554
  219.9 2.9 %collective-permute-start.57 = (bf16[120,768]{1,0:T(8,128)(2,1)S(1)}, bf16[120,768]{1,0:T(8,128)(2,1)S(1)}, u32[]{:S(2)}, u32[]{:S(2)}) collective-permute-start(bf16[120,768]{1,0:T(8,128)(2,1)S(1)} %get-tuple-element.277), channel_id=1, source_target_pairs={{0,8},{4,12},{8,0},{12,4},{16,24},{20,28},{24,16},{28,20},{1,9},{5... | collective-permute-start | bytes 552968 | tf_op jit(solution)/shard_map/ppermute | solution.py:554
  222.8 2.9 %collective-permute-start.58 = (bf16[120,768]{1,0:T(8,128)(2,1)S(1)}, bf16[120,768]{1,0:T(8,128)(2,1)S(1)}, u32[]{:S(2)}, u32[]{:S(2)}) collective-permute-start(bf16[120,768]{1,0:T(8,128)(2,1)S(1)} %get-tuple-element.277), channel_id=1, source_target_pairs={{0,16},{4,20},{8,24},{12,28},{16,0},{20,4},{24,8},{28,12},{1,17},{... | collective-permute-start | bytes 552968 | tf_op jit(solution)/shard_map/ppermute | solution.py:554
  228.5 10.9 %collective-permute-done.52 = bf16[80,768]{1,0:T(8,128)(2,1)S(1)} collective-permute-done((bf16[80,768]{1,0:T(8,128)(2,1)S(1)}, bf16[80,768]{1,0:T(8,128)(2,1)S(1)}, u32[]{:S(2)}, u32[]{:S(2)}) %collective-permute-start.52) | collective-permute-done | bytes 122912 | tf_op jit(solution)/shard_map/ppermute | solution.py:554
  241.5 4.4 %collective-permute-done.59 = bf16[120,768]{1,0:T(8,128)(2,1)S(1)} collective-permute-done((bf16[120,768]{1,0:T(8,128)(2,1)S(1)}, bf16[120,768]{1,0:T(8,128)(2,1)S(1)}, u32[]{:S(2)}, u32[]{:S(2)}) %collective-permute-start.59) | collective-permute-done | bytes 184352 | tf_op jit(solution)/shard_map/ppermute | solution.py:554
  253.2 10.9 %collective-permute-done.60 = bf16[480,768]{1,0:T(8,128)(2,1)S(1)} collective-permute-done((bf16[480,768]{1,0:T(8,128)(2,1)S(1)}, bf16[480,768]{1,0:T(8,128)(2,1)S(1)}, u32[]{:S(2)}, u32[]{:S(2)}) %collective-permute-start.60) | collective-permute-done | bytes 737312 | tf_op jit(solution)/shard_map/ppermute | solution.py:554
  (304 shorter events, 84.4 us)
Async XLA Ops:
  0.7 22.4 %collective-permute-start.2 = (bf16[3,192,768]{2,1,0:T(8,128)(2,1)}, bf16[3,192,768]{2,1,0:T(8,128)(2,1)}, u32[]{:S(2)}, u32[]{:S(2)}) collective-permute-start(bf16[3,192,768]{2,1,0:T(8,128)(2,1)} %bitcast.30), channel_id=1, source_target_pairs={{0,2},{1,3},{2,0},{3,1},{4,6},{5,7},{6,4},{7,5},{8,10},{9,11},{10,... | collective-permute-start | bytes 2654216 | tf_op jit(solution)/shard_map/ppermute | solution.py:554
  2.5 20.7 %collective-permute-start.3 = (f32[2,192]{1,0:T(2,128)}, f32[2,192]{1,0:T(2,128)S(1)}, u32[]{:S(2)}, u32[]{:S(2)}) collective-permute-start(f32[2,192]{1,0:T(2,128)} %b_one.1), channel_id=1, source_target_pairs={{0,2},{1,3},{2,0},{3,1},{4,6},{5,7},{6,4},{7,5},{8,10},{9,11},{10,... | collective-permute-start | bytes 4616 | tf_op jit(solution)/shard_map/ppermute | solution.py:554
  25.7 22.8 %collective-permute-start.11 = (bf16[768,768]{1,0:T(8,128)(2,1)S(1)}, bf16[768,768]{1,0:T(8,128)(2,1)S(1)}, u32[]{:S(2)}, u32[]{:S(2)}) collective-permute-start(bf16[768,768]{1,0:T(8,128)(2,1)S(1)} %copy-done.8), channel_id=1, source_target_pairs={{0,1},{1,0},{2,3},{3,2},{4,5},{5,4},{6,7},{7,6},{8,9},{9,8},{10,11... | collective-permute-start | bytes 3538952 | tf_op jit(solution)/shard_map/ppermute | solution.py:554
  27.2 19.8 %collective-permute-start.10 = (bf16[384,768]{1,0:T(8,128)(2,1)S(1)}, bf16[384,768]{1,0:T(8,128)(2,1)S(1)}, u32[]{:S(2)}, u32[]{:S(2)}) collective-permute-start(bf16[384,768]{1,0:T(8,128)(2,1)S(1)} %constant_dynamic-slice_fusion.22), channel_id=1, source_target_pairs={{0,2},{1,3},{2,0},{3,1},{4,6},{5,7},{6,4},{7,5},{8,10},{9,11},{10,... | collective-permute-start | bytes 1769480 | tf_op jit(solution)/shard_map/ppermute | solution.py:554
  28.8 19.7 %collective-permute-start.12 = (bf16[768,768]{1,0:T(8,128)(2,1)S(1)}, bf16[768,768]{1,0:T(8,128)(2,1)S(1)}, u32[]{:S(2)}, u32[]{:S(2)}) collective-permute-start(bf16[768,768]{1,0:T(8,128)(2,1)S(1)} %copy-done.15), channel_id=1, source_target_pairs={{0,1},{1,0},{2,3},{3,2},{4,5},{5,4},{6,7},{7,6},{8,9},{9,8},{10,11... | collective-permute-start | bytes 3538952 | tf_op jit(solution)/shard_map/ppermute | solution.py:554
  42.9 29.0 %collective-permute-start.16 = (bf16[768,768]{1,0:T(8,128)(2,1)S(1)}, bf16[768,768]{1,0:T(8,128)(2,1)}, u32[]{:S(2)}, u32[]{:S(2)}) collective-permute-start(bf16[768,768]{1,0:T(8,128)(2,1)S(1)} %copy-done.15), channel_id=1, source_target_pairs={{0,2},{1,3},{2,0},{3,1},{4,6},{5,7},{6,4},{7,5},{8,10},{9,11},{10,... | collective-permute-start | bytes 3538952 | tf_op jit(solution)/shard_map/ppermute | solution.py:554
  47.0 21.5 %collective-permute-start.14 = (bf16[384,768]{1,0:T(8,128)(2,1)S(1)}, bf16[384,768]{1,0:T(8,128)(2,1)}, u32[]{:S(2)}, u32[]{:S(2)}) collective-permute-start(bf16[384,768]{1,0:T(8,128)(2,1)S(1)} %collective-permute-done.10.refs_0_), channel_id=1, source_target_pairs={{0,4},{4,0},{8,12},{12,8},{16,20},{20,16},{24,28},{28,24},{1,5},{5... | collective-permute-start | bytes 1769480 | tf_op jit(solution)/shard_map/ppermute | solution.py:554
  48.5 20.0 %collective-permute-start.15 = (bf16[384,768]{1,0:T(8,128)(2,1)S(1)}, bf16[384,768]{1,0:T(8,128)(2,1)S(1)}, u32[]{:S(2)}, u32[]{:S(2)}) collective-permute-start(bf16[384,768]{1,0:T(8,128)(2,1)S(1)} %collective-permute-done.10.refs_0_), channel_id=1, source_target_pairs={{0,1},{1,0},{2,3},{3,2},{4,5},{5,4},{6,7},{7,6},{8,9},{9,8},{10,11... | collective-permute-start | bytes 1769480 | tf_op jit(solution)/shard_map/ppermute | solution.py:554
  73.5 21.8 %collective-permute-start.20 = (bf16[768,768]{1,0:T(8,128)(2,1)}, bf16[768,768]{1,0:T(8,128)(2,1)S(1)}, u32[]{:S(2)}, u32[]{:S(2)}) collective-permute-start(bf16[768,768]{1,0:T(8,128)(2,1)} %copy-done.20), channel_id=1, source_target_pairs={{0,1},{1,0},{2,3},{3,2},{4,5},{5,4},{6,7},{7,6},{8,9},{9,8},{10,11... | collective-permute-start | bytes 3538952 | tf_op jit(solution)/shard_map/ppermute | solution.py:554
  74.1 21.2 %collective-permute-start.21 = (bf16[768,768]{1,0:T(8,128)(2,1)}, bf16[768,768]{1,0:T(8,128)(2,1)S(1)}, u32[]{:S(2)}, u32[]{:S(2)}) collective-permute-start(bf16[768,768]{1,0:T(8,128)(2,1)} %copy-done.19), channel_id=1, source_target_pairs={{0,1},{1,0},{2,3},{3,2},{4,5},{5,4},{6,7},{7,6},{8,9},{9,8},{10,11... | collective-permute-start | bytes 3538952 | tf_op jit(solution)/shard_map/ppermute | solution.py:554
  118.6 18.4 %collective-permute-start.28 = (bf16[640,768]{1,0:T(8,128)(2,1)S(1)}, bf16[640,768]{1,0:T(8,128)(2,1)S(1)}, u32[]{:S(2)}, u32[]{:S(2)}) collective-permute-start(bf16[640,768]{1,0:T(8,128)(2,1)S(1)} %fusion.5), channel_id=1, source_target_pairs={{0,1},{1,0},{2,3},{3,2},{4,5},{5,4},{6,7},{7,6},{8,9},{9,8},{10,11... | collective-permute-start | bytes 2949128 | tf_op jit(solution)/shard_map/ppermute | solution.py:554
  122.8 20.5 %collective-permute-start.32 = (bf16[192,768]{1,0:T(8,128)(2,1)S(1)}, bf16[192,768]{1,0:T(8,128)(2,1)S(1)}, u32[]{:S(2)}, u32[]{:S(2)}) collective-permute-start(bf16[192,768]{1,0:T(8,128)(2,1)S(1)} %get-tuple-element.315), channel_id=1, source_target_pairs={{0,4},{4,0},{8,12},{12,8},{16,20},{20,16},{24,28},{28,24},{1,5},{5... | collective-permute-start | bytes 884744 | tf_op jit(solution)/shard_map/ppermute | solution.py:554
  123.9 32.5 %collective-permute-start.33 = (bf16[576,768]{1,0:T(8,128)(2,1)S(1)}, bf16[576,768]{1,0:T(8,128)(2,1)S(1)}, u32[]{:S(2)}, u32[]{:S(2)}) collective-permute-start(bf16[576,768]{1,0:T(8,128)(2,1)S(1)} %pad_maximum_fusion.4), channel_id=1, source_target_pairs={{0,2},{1,3},{2,0},{3,1},{4,6},{5,7},{6,4},{7,5},{8,10},{9,11},{10,... | collective-permute-start | bytes 2654216 | tf_op jit(solution)/shard_map/ppermute | solution.py:554
  137.4 19.1 %collective-permute-start.31 = (bf16[320,768]{1,0:T(8,128)(2,1)S(1)}, bf16[320,768]{1,0:T(8,128)(2,1)S(1)}, u32[]{:S(2)}, u32[]{:S(2)}) collective-permute-start(bf16[320,768]{1,0:T(8,128)(2,1)S(1)} %get-tuple-element.302), channel_id=1, source_target_pairs={{0,4},{4,0},{8,12},{12,8},{16,20},{20,16},{24,28},{28,24},{1,5},{5... | collective-permute-start | bytes 1474568 | tf_op jit(solution)/shard_map/ppermute | solution.py:554
  139.3 17.2 %collective-permute-start.34 = (bf16[96,768]{1,0:T(8,128)(2,1)S(1)}, bf16[96,768]{1,0:T(8,128)(2,1)S(1)}, u32[]{:S(2)}, u32[]{:S(2)}) collective-permute-start(bf16[96,768]{1,0:T(8,128)(2,1)S(1)} %get-tuple-element.313), channel_id=1, source_target_pairs={{0,8},{4,12},{8,0},{12,4},{16,24},{20,28},{24,16},{28,20},{1,9},{5... | collective-permute-start | bytes 442376 | tf_op jit(solution)/shard_map/ppermute | solution.py:554
  165.0 20.1 %collective-permute-start.38 = (bf16[320,768]{1,0:T(8,128)(2,1)S(1)}, bf16[320,768]{1,0:T(8,128)(2,1)S(1)}, u32[]{:S(2)}, u32[]{:S(2)}) collective-permute-start(bf16[320,768]{1,0:T(8,128)(2,1)S(1)} %get-tuple-element.300), channel_id=1, source_target_pairs={{0,4},{4,0},{8,12},{12,8},{16,20},{20,16},{24,28},{28,24},{1,5},{5... | collective-permute-start | bytes 1474568 | tf_op jit(solution)/shard_map/ppermute | solution.py:554
  185.4 32.7 %collective-permute-start.56 = (bf16[120,768]{1,0:T(8,128)(2,1)S(1)}, bf16[120,768]{1,0:T(8,128)(2,1)S(1)}, u32[]{:S(2)}, u32[]{:S(2)}) collective-permute-start(bf16[120,768]{1,0:T(8,128)(2,1)S(1)} %get-tuple-element.309), channel_id=1, source_target_pairs={{0,24},{4,28},{8,16},{12,20},{16,8},{20,12},{24,0},{28,4},{1,25},{... | collective-permute-start | bytes 552968 | tf_op jit(solution)/shard_map/ppermute | solution.py:554
  186.0 32.2 %collective-permute-start.55 = (bf16[120,768]{1,0:T(8,128)(2,1)S(1)}, bf16[120,768]{1,0:T(8,128)(2,1)S(1)}, u32[]{:S(2)}, u32[]{:S(2)}) collective-permute-start(bf16[120,768]{1,0:T(8,128)(2,1)S(1)} %get-tuple-element.310), channel_id=1, source_target_pairs={{0,16},{4,20},{8,24},{12,28},{16,0},{20,4},{24,8},{28,12},{1,17},{... | collective-permute-start | bytes 552968 | tf_op jit(solution)/shard_map/ppermute | solution.py:554
  212.9 33.7 %collective-permute-start.61 = (bf16[384,768]{1,0:T(8,128)(2,1)S(1)}, bf16[384,768]{1,0:T(8,128)(2,1)S(1)}, u32[]{:S(2)}, u32[]{:S(2)}) collective-permute-start(bf16[384,768]{1,0:T(8,128)(2,1)S(1)} %constant_dynamic-update-slice_fusion.5), channel_id=1, source_target_pairs={{0,4},{4,0},{8,12},{12,8},{16,20},{20,16},{24,28},{28,24},{1,5},{5... | collective-permute-start | bytes 1769480 | tf_op jit(solution)/shard_map/ppermute | solution.py:554
  218.1 21.3 %collective-permute-start.52 = (bf16[80,768]{1,0:T(8,128)(2,1)S(1)}, bf16[80,768]{1,0:T(8,128)(2,1)S(1)}, u32[]{:S(2)}, u32[]{:S(2)}) collective-permute-start(bf16[80,768]{1,0:T(8,128)(2,1)S(1)} %get-tuple-element.279), channel_id=1, source_target_pairs={{0,24},{4,28},{8,16},{12,20},{16,8},{20,12},{24,0},{28,4},{1,25},{... | collective-permute-start | bytes 368648 | tf_op jit(solution)/shard_map/ppermute | solution.py:554
  219.9 20.3 %collective-permute-start.57 = (bf16[120,768]{1,0:T(8,128)(2,1)S(1)}, bf16[120,768]{1,0:T(8,128)(2,1)S(1)}, u32[]{:S(2)}, u32[]{:S(2)}) collective-permute-start(bf16[120,768]{1,0:T(8,128)(2,1)S(1)} %get-tuple-element.277), channel_id=1, source_target_pairs={{0,8},{4,12},{8,0},{12,4},{16,24},{20,28},{24,16},{28,20},{1,9},{5... | collective-permute-start | bytes 552968 | tf_op jit(solution)/shard_map/ppermute | solution.py:554
  222.8 18.7 %collective-permute-start.58 = (bf16[120,768]{1,0:T(8,128)(2,1)S(1)}, bf16[120,768]{1,0:T(8,128)(2,1)S(1)}, u32[]{:S(2)}, u32[]{:S(2)}) collective-permute-start(bf16[120,768]{1,0:T(8,128)(2,1)S(1)} %get-tuple-element.277), channel_id=1, source_target_pairs={{0,16},{4,20},{8,24},{12,28},{16,0},{20,4},{24,8},{28,12},{1,17},{... | collective-permute-start | bytes 552968 | tf_op jit(solution)/shard_map/ppermute | solution.py:554
  226.8 19.1 %collective-permute-start.59 = (bf16[120,768]{1,0:T(8,128)(2,1)S(1)}, bf16[120,768]{1,0:T(8,128)(2,1)S(1)}, u32[]{:S(2)}, u32[]{:S(2)}) collective-permute-start(bf16[120,768]{1,0:T(8,128)(2,1)S(1)} %get-tuple-element.277), channel_id=1, source_target_pairs={{0,24},{4,28},{8,16},{12,20},{16,8},{20,12},{24,0},{28,4},{1,25},{... | collective-permute-start | bytes 552968 | tf_op jit(solution)/shard_map/ppermute | solution.py:554
  246.0 18.2 %collective-permute-start.60 = (bf16[480,768]{1,0:T(8,128)(2,1)S(1)}, bf16[480,768]{1,0:T(8,128)(2,1)S(1)}, u32[]{:S(2)}, u32[]{:S(2)}) collective-permute-start(bf16[480,768]{1,0:T(8,128)(2,1)S(1)} %constant_dynamic-update-slice_fusion.9), channel_id=1, source_target_pairs={{0,4},{4,0},{8,12},{12,8},{16,20},{20,16},{24,28},{28,24},{1,5},{5... | collective-permute-start | bytes 2211848 | tf_op jit(solution)/shard_map/ppermute | solution.py:554
  (88 other events, 833.3 us)
